TPU v7x, 512 devices: a whole 4x8x8 slice. The times are simulated.
512 devices in a mesh: tile: 64 (over y, z_lo, core), img: 8 (over z_hi, x).
Axes of the slice: x: 4, y: 8, z: 8 (z_hi: 2, z_lo: 4; z = z_hi * 4 + z_lo), core: 2. Of those that a mesh axis runs over, the one named last changes fastest.
Arguments:
- heights: float32 [64, 64, 128], P('tile'), may hold values from -1.5 to 1.5
- albedo: float32 [64, 64, 128], P('tile'), may hold values from 0.5 to 1.5
- blocks: bfloat16 [64, 8, 64, 64, 128], P('tile', 'img'), may hold values from 0 to 1
- block_params: bfloat16 [64, 8, 64, 8], P('tile', 'img'), may hold values from -1 to 2, as said below
- block_dest: int32 [64, 8, 64, 1], P('tile', 'img'), may hold values from 0 to 63; in each aligned block of 64 rows (0 to 63, 64 to 127, ..., all dimensions but the last counted through in order) at most 2 rows name the same one
Outputs:
- grad_heights: float32 [64, 64, 128], P('tile', 'img')
- grad_albedo: float32 [64, 64, 128], P('tile', 'img')
Inputs may be any that keep to these rules, and one draw needn't show every extreme that they name: `block_params`: columns 0 to 2 are a unit sun vector whose third entry lies between 0.05 and 0.43, columns 3 to 5 a unit view vector whose first two entries lie within -0.15 and 0.15, column 6 lies between 0.2 and 0.9 and column 7 between 0.5 and 2. `block_dest`: of the blocks held by one device, at most 2 lie on any one tile, and in every draw some device holds exactly 2 blocks of some tile.
All inputs are finite; a program needn't handle non-finite values.
Results may differ from a plain program's by a relative error of at most 0.0003.
Values may be sent and summed in bfloat16 or wider, within the bound.
No kernel may reach another device: no remote copies, remote signals or barrier semaphores. Data moves between devices by JAX's collectives and lax.ppermute only.
A program may use at most 64 MiB of HBM per device.

v0:
```python
import jax
import jax.numpy as jnp
from jax import lax
from jax.experimental import pallas as pl
from jax.experimental.pallas import tpu as pltpu
from jax.sharding import Mesh
from jax.sharding import PartitionSpec as P


SMOOTH = 0.0025
PARAMS = 8
STRIP = 16
ROWS, CLASSES, CORES, HALVES, DEPTH = 8, 4, 2, 2, 4
RING = CLASSES * HALVES
TILE = ("y", "zl", "c")
IMG = ("zh", "x")

SMEM = pl.BlockSpec(memory_space=pltpu.SMEM)
VMEM = pl.BlockSpec(memory_space=pltpu.VMEM)


def ring_shift(value, steps):
    pairs = []
    for low in range(CLASSES):
        for core in range(CORES):
            for high in range(HALVES):
                z = (high * CLASSES + low + steps) % RING
                source = (low * CORES + core) * HALVES + high
                pairs.append((source, ((z % CLASSES) * CORES + core) * HALVES + z // CLASSES))
    return lax.ppermute(value, ("zl", "c", "zh"), pairs)


def column_shift(value, steps):
    count = CLASSES * CORES
    pairs = [(k, k + steps) for k in range(count) if 0 <= k + steps < count]
    return lax.ppermute(value, ("zl", "c"), pairs)


def in_vmem(*arrays):
    return [pltpu.with_memory_space_constraint(a, pltpu.VMEM) for a in arrays]


def fill_table(dest_ref, table):
    def clear(index, carry):
        table[index] = -1
        return carry

    lax.fori_loop(0, table.shape[0], clear, 0, unroll=8)

    def note(index, carry):
        place = dest_ref[index] * 2
        second = (table[place] >= 0).astype(jnp.int32)
        table[place + second] = index
        return carry

    lax.fori_loop(0, dest_ref.shape[0], note, 0, unroll=4)


def pack_kernel(here_ref, dest_ref, params_ref, blocks_ref, near_ref, own_ref, other_ref, table, lines):
    tile_rows = blocks_ref.shape[1]
    fill_table(dest_ref, table)
    low, core = here_ref[0], here_ref[1]

    def target(kind, d):
        if kind == 1:
            return other_ref.at[d]
        return near_ref if d == 0 else own_ref.at[d - 1]

    for kind in range(CORES):
        for d in range(CLASSES):
            column = ((low + d) % CLASSES) * CORES + (core + kind) % CORES
            unit = target(kind, d)

            def place(row, carry):
                tile = row * (CLASSES * CORES) + column
                for slot in (0, 1):
                    block = table[2 * tile + slot]
                    kept = block >= 0
                    block = jnp.maximum(block, 0)
                    values = blocks_ref[block]
                    first = pl.multiple_of(row * tile_rows, tile_rows)
                    unit[slot, pl.ds(first, tile_rows), :] = jnp.where(kept, values, jnp.zeros_like(values))
                    lines[slot, pl.ds(row, 1), :] = jnp.where(kept, params_ref[pl.ds(block, 1), :], 0.0)
                return carry

            lax.fori_loop(0, ROWS, place, 0)
            for slot in (0, 1):
                unit[slot, ROWS * tile_rows :, :] = lines[slot].astype(unit.dtype)


def pack(here, dest, params_wide, blocks):
    _, tile_rows, tile_cols = blocks.shape
    unit = (2, ROWS * tile_rows + ROWS, tile_cols)
    return pl.pallas_call(
        pack_kernel,
        out_shape=[pltpu.VMEM(lead + unit, jnp.bfloat16) for lead in ((), (CLASSES - 1,), (CLASSES,))],
        in_specs=[SMEM, SMEM, VMEM, VMEM],
        out_specs=[VMEM] * 3,
        scratch_shapes=[
            pltpu.SMEM((2 * ROWS * CLASSES * CORES,), jnp.int32),
            pltpu.VMEM((2, ROWS, tile_cols), jnp.float32),
        ],
        cost_estimate=pl.CostEstimate(flops=0, bytes_accessed=6 << 20, transcendentals=0),
        compiler_params=pltpu.CompilerParams(vmem_limit_bytes=4 << 20),
        name="pack",
    )(here, dest, *in_vmem(params_wide, blocks))


def terms_kernel(scale, with_sums, picks, *refs):
    maps_ref, *refs = refs
    sums_ref = None
    if with_sums:
        sums_ref, *refs = refs
    *got, out_ref, lines, params, sem = refs
    units = [ref.at[pick] for ref, some in zip(got, picks) for pick in some]
    pixels = maps_ref.shape[1]
    for index, unit in enumerate(units):
        lines[index * ROWS : (index + 1) * ROWS, :] = unit[pixels:, :].astype(jnp.float32)
    copy = pltpu.make_async_copy(lines, params, sem)
    copy.start()
    copy.wait()

    def strip(index, carry):
        first = pl.multiple_of(index * STRIP, STRIP)
        part = pl.ds(first, STRIP)
        row = index // (pixels // ROWS // STRIP)
        p, q, w, albedo = (maps_ref[k, part, :] for k in range(4))
        pw = p * w
        qw = q * w
        if with_sums:
            sum_x, sum_y, sum_z, shade = (sums_ref[k, part, :] for k in range(4))
        else:
            sum_x = sum_y = sum_z = shade = jnp.zeros((STRIP, maps_ref.shape[2]), jnp.float32)
        for number, unit in enumerate(units):
            sx, sy, sz, vx, vy, vz, mix, gain = [params[number * ROWS + row, k] for k in range(PARAMS)]
            mix2 = mix * 2.0
            rest = 1.0 - mix
            bright = unit[part, :].astype(jnp.float32)
            ci = sz * w - sx * pw - sy * qw
            ce = vz * w - vx * pw - vy * qw
            square = ci * ci + SMOOTH
            inv_root = lax.rsqrt(square)
            mu = (ci + square * inv_root) * 0.5
            inv = 1.0 / (mu + ce)
            k = mix2 * inv
            u = mu * inv
            c = ce * inv
            shading = mu * (k + rest)
            misfit = (gain * albedo) * shading - bright
            scaled = gain * misfit
            shade = shade + scaled * shading
            gs = scaled * albedo
            gk = gs * k
            gl = gk * c + gs * rest
            gi = gl * (mu * inv_root)
            ge = gk * u
            sum_x = sum_x + (gi * sx - ge * vx)
            sum_y = sum_y + (gi * sy - ge * vy)
            sum_z = sum_z + (gi * sz - ge * vz)
        if scale is None:
            for k, total in enumerate((sum_x, sum_y, sum_z, shade)):
                out_ref[k, part, :] = total
        else:
            up = (w * w * w) * (sum_z - p * sum_x - q * sum_y)
            out_ref[0, part, :] = (-(w * sum_x) - p * up) * (0.5 * scale)
            out_ref[1, part, :] = (-(w * sum_y) - q * up) * (0.5 * scale)
            out_ref[2, part, :] = shade * scale
        return carry

    lax.fori_loop(0, pixels // STRIP, strip, 0)


def terms(maps, sums, got, scale):
    arrays, picks = zip(*got)
    count = sum(len(some) for some in picks)
    given = [maps] + ([] if sums is None else [sums]) + list(arrays)
    pixels, cols = maps.shape[1:]
    return pl.pallas_call(
        lambda *refs: terms_kernel(scale, sums is not None, picks, *refs),
        out_shape=pltpu.VMEM((4 if scale is None else 3, pixels, cols), jnp.float32),
        in_specs=[VMEM] * len(given),
        out_specs=VMEM,
        scratch_shapes=[
            pltpu.VMEM((count * ROWS, cols), jnp.float32),
            pltpu.SMEM((count * ROWS, cols), jnp.float32),
            pltpu.SemaphoreType.DMA,
        ],
        cost_estimate=pl.CostEstimate(flops=60 * count * pixels * cols, bytes_accessed=4 << 20, transcendentals=0),
        compiler_params=pltpu.CompilerParams(vmem_limit_bytes=4 << 20),
    )(*in_vmem(*given))


EACH2 = [(0,), (1,)]
EACH4 = EACH2 + [(2,), (3,)]


def body(heights, albedo, blocks, block_params, block_dest):
    column_here = lax.axis_index(("zl", "c"))
    last_column = CLASSES * CORES - 1
    tile_rows, tile_cols = heights.shape[1:]
    block_count = block_dest.shape[2]
    pixels = ROWS * tile_rows

    params_wide = jnp.pad(
        block_params.reshape(block_count, PARAMS).astype(jnp.float32), ((0, 0), (0, tile_cols - PARAMS))
    )
    here = jnp.stack([lax.axis_index("zl"), lax.axis_index("c")]).astype(jnp.int32)
    near, own, other = pack(
        here,
        block_dest.reshape(block_count),
        params_wide,
        blocks.reshape(block_count, tile_rows, tile_cols),
    )
    swapped = lax.ppermute(other, "c", [(0, 1), (1, 0)])
    to_right = jnp.concatenate([own[0], swapped[1]])
    to_left = jnp.concatenate([own[2], swapped[3]])
    to_right2 = jnp.stack([own[1, 0], swapped[2, 0]])
    to_left2 = jnp.stack([own[1, 1], swapped[2, 1]])
    right = ring_shift(to_right, 1)
    left = ring_shift(to_left, -1)
    right2 = ring_shift(to_right2, 2)
    left2 = ring_shift(to_left2, -2)

    here_maps = jnp.concatenate([heights[0], albedo[0]])
    copies = jnp.broadcast_to(here_maps[None], (ROWS,) + here_maps.shape)
    gathered = lax.all_to_all(copies, "y", split_axis=0, concat_axis=0, tiled=True)
    height = gathered[:, :tile_rows].reshape(pixels, tile_cols)
    albedo_map = gathered[:, tile_rows:].reshape(pixels, tile_cols)
    first_column, final_column = height[:, 0], height[:, -1]
    from_west = column_shift(final_column, 1)
    from_east = column_shift(first_column, -1)
    west = jnp.where(column_here > 0, from_west, first_column)
    east = jnp.where(column_here < last_column, from_east, final_column)
    widened = jnp.concatenate([west[:, None], height, east[:, None]], axis=1)
    taller = jnp.concatenate([height[:1], height, height[-1:]], axis=0)
    slope_x = (widened[:, 2:] - widened[:, :-2]) * 0.5
    slope_y = (taller[2:] - taller[:-2]) * 0.5
    shrink = 1.0 / jnp.sqrt(1.0 + slope_x * slope_x + slope_y * slope_y)
    maps = jnp.stack([slope_x, slope_y, shrink, albedo_map])

    sums = terms(maps, None, [(near, [(0,), (1,)]), (swapped, [(0, 0), (0, 1)])], None)
    sums = terms(maps, sums, [(right, EACH4), (left, EACH4)], None)
    half_x, half_y, albedo_grad = terms(maps, sums, [(right2, EACH2), (left2, EACH2)], 1.0 / block_count)

    before = jnp.where(column_here == 0, -half_x[:, 0], column_shift(half_x[:, -1], 1))
    after = jnp.where(column_here == last_column, -half_x[:, -1], column_shift(half_x[:, 0], -1))
    wide = jnp.concatenate([before[:, None], half_x, after[:, None]], axis=1)
    tall = jnp.concatenate([-half_y[:1], half_y, -half_y[-1:]], axis=0)
    height_grad = wide[:, :-2] - wide[:, 2:] + tall[:-2] - tall[2:]
    groups = HALVES * DEPTH
    parts = [g.reshape(ROWS * groups, 1, tile_rows // groups, tile_cols) for g in (height_grad, albedo_grad)]
    swapped_parts = lax.all_to_all(
        jnp.concatenate(parts, axis=1), ("y",) + IMG, split_axis=0, concat_axis=0, tiled=True
    )
    summed = jnp.sum(swapped_parts, axis=0)
    return (summed[:1], summed[1:])


def solution(mesh):
    physical = Mesh(mesh.devices.reshape(ROWS, CLASSES, CORES, HALVES, DEPTH), TILE + IMG)
    placed = (
        P(TILE, None, None),
        P(TILE, None, None),
        P(TILE, IMG, None, None, None),
        P(TILE, IMG, None, None),
        P(TILE, IMG, None, None),
    )

    return jax.shard_map(
        body,
        mesh=physical,
        in_specs=placed,
        out_specs=(P(TILE, IMG, None), P(TILE, IMG, None)),
        check_vma=False,
    )
```

profile of v0, /device:TPU:1, one launch (start us, length us, event | category | flops | bytes accessed | tf_op | source)
XLA Modules:
  0.0 114.4 jit_solution(11016812142185833475)
XLA Ops:
  0.7 0.9 pad_maximum_fusion.14
  1.5 0.8 broadcast_in_dim.18
  2.4 7.6 %all-to-all-start = ((f32[8,128,128]{2,1,0:T(8,128)}), f32[8,128,128]{2,1,0:T(8,128)S(1)}, u32[]{:S(2)}, u32[]{:S(2)}) async-start(f32[8,128,128]{2,1,0:T(8,128)} %broadcast_in_dim.18), calls=%async_computation | async-start | bytes 1048576 | tf_op jit(solution)/shard_map/all_to_all | solution.py:226
  10.2 2.4 %pack.1 = (bf16[2,520,128]{2,1,0:T(8,128)(2,1)S(1)}, bf16[3,2,520,128]{3,2,1,0:T(8,128)(2,1)S(1)}, bf16[4,2,520,128]{3,2,1,0:T(8,128)(2,1)S(1)}) custom-call(s32[2]{0:T(128)S(1)} %pad_add_fusion.here_ref, s32[64]{0:T(128)S(1)} %bitcast.52, f32[64,128]{1,0:T(8,128)S(1)} %pad_convert_fusion.params_ref, bf16[64,64,128]{2,1,0:T(8,128)(2,1)S(1)} %bitcast.51), custom_call_target="tpu_custom_call" | custom-call | bytes 6291456 | tf_op jit(solution)/shard_map/pack/pallas_call | solution.py:94
  12.7 4.6 %collective-permute-start.2 = (bf16[4,2,520,128]{3,2,1,0:T(8,128)(2,1)S(1)}, bf16[4,2,520,128]{3,2,1,0:T(8,128)(2,1)S(1)}, u32[]{:S(2)}, u32[]{:S(2)}) collective-permute-start(bf16[4,2,520,128]{3,2,1,0:T(8,128)(2,1)S(1)} %get-tuple-element.6), channel_id=1, source_target_pairs={{0,8},{8,0},{1,9},{9,1},{2,10},{10,2},{3,11},{11,3},{4,12},{12,4},... | collective-permute-start | bytes 3194888 | tf_op jit(solution)/shard_map/ppermute | solution.py:214
  17.3 0.7 slice_bitcast_fusion.2
  18.0 0.7 slice_bitcast_fusion.9
  18.8 6.2 %all-to-all-done = f32[8,128,128]{2,1,0:T(8,128)S(1)} async-done(((f32[8,128,128]{2,1,0:T(8,128)}), f32[8,128,128]{2,1,0:T(8,128)S(1)}, u32[]{:S(2)}, u32[]{:S(2)}) %all-to-all-start) | async-done | bytes 524320 | tf_op jit(solution)/shard_map/all_to_all | solution.py:226
  25.0 0.7 fusion.12
  25.7 0.3 slice_reduce_fusion.3
  26.0 7.4 %collective-permute-start.1 = (f32[512]{0:T(512)S(1)}, f32[512]{0:T(512)S(1)}, u32[]{:S(2)}, u32[]{:S(2)}) collective-permute-start(f32[512]{0:T(512)S(1)} %get-tuple-element.11), channel_id=1, source_target_pairs={{0,8},{8,16},{16,24},{24,32},{32,40},{40,48},{48,56},{1,9},{9,17},... | collective-permute-start | bytes 6152 | tf_op jit(solution)/shard_map/ppermute | solution.py:36
  33.4 1.9 %collective-permute-start = (f32[512]{0:T(512)S(1)}, f32[512]{0:T(512)S(1)}, u32[]{:S(2)}, u32[]{:S(2)}) collective-permute-start(f32[512]{0:T(512)S(1)} %get-tuple-element.10), channel_id=1, source_target_pairs={{8,0},{16,8},{24,16},{32,24},{40,32},{48,40},{56,48},{9,1},{17,9},... | collective-permute-start | bytes 6152 | tf_op jit(solution)/shard_map/ppermute | solution.py:36
  35.4 0.8 copy.14
  36.2 2.1 %collective-permute-done = f32[512]{0:T(512)S(1)} collective-permute-done((f32[512]{0:T(512)S(1)}, f32[512]{0:T(512)S(1)}, u32[]{:S(2)}, u32[]{:S(2)}) %collective-permute-start) | collective-permute-done | bytes 2080 | tf_op jit(solution)/shard_map/ppermute | solution.py:36
  38.3 0.9 copy.13
  39.3 4.1 %collective-permute-start.3 = (bf16[4,520,128]{2,1,0:T(8,128)(2,1)S(1)}, bf16[4,520,128]{2,1,0:T(8,128)(2,1)S(1)}, u32[]{:S(2)}, u32[]{:S(2)}) collective-permute-start(bf16[4,520,128]{2,1,0:T(8,128)(2,1)S(1)} %pad_maximum_fusion.1), channel_id=1, source_target_pairs={{0,16},{4,20},{8,24},{12,28},{16,32},{20,36},{24,40},{28,44},{32,4... | collective-permute-start | bytes 1597448 | tf_op jit(solution)/shard_map/ppermute | solution.py:30
  43.5 4.6 %collective-permute-start.4 = (bf16[4,520,128]{2,1,0:T(8,128)(2,1)S(1)}, bf16[4,520,128]{2,1,0:T(8,128)(2,1)S(1)}, u32[]{:S(2)}, u32[]{:S(2)}) collective-permute-start(bf16[4,520,128]{2,1,0:T(8,128)(2,1)S(1)} %pad_maximum_fusion.2), channel_id=1, source_target_pairs={{0,52},{4,48},{8,60},{12,56},{16,0},{20,4},{24,8},{28,12},{32,16},... | collective-permute-start | bytes 1597448 | tf_op jit(solution)/shard_map/ppermute | solution.py:30
  48.3 2.7 %collective-permute-start.5 = (bf16[2,520,128]{2,1,0:T(8,128)(2,1)S(1)}, bf16[2,520,128]{2,1,0:T(8,128)(2,1)S(1)}, u32[]{:S(2)}, u32[]{:S(2)}) collective-permute-start(bf16[2,520,128]{2,1,0:T(8,128)(2,1)S(1)} %pad_maximum_fusion.4), channel_id=1, source_target_pairs={{0,32},{4,36},{8,40},{12,44},{16,48},{20,52},{24,56},{28,60},{32,4... | collective-permute-start | bytes 798728 | tf_op jit(solution)/shard_map/ppermute | solution.py:30
  51.0 5.9 %collective-permute-start.6 = (bf16[2,520,128]{2,1,0:T(8,128)(2,1)S(1)}, bf16[2,520,128]{2,1,0:T(8,128)(2,1)S(1)}, u32[]{:S(2)}, u32[]{:S(2)}) collective-permute-start(bf16[2,520,128]{2,1,0:T(8,128)(2,1)S(1)} %pad_maximum_fusion.5), channel_id=1, source_target_pairs={{0,36},{4,32},{8,44},{12,40},{16,52},{20,48},{24,60},{28,56},{32,0... | collective-permute-start | bytes 798728 | tf_op jit(solution)/shard_map/ppermute | solution.py:30
  56.9 0.3 fusion.9
  57.3 3.2 %shard_map.68.refs_1_ = f32[4,512,128]{2,1,0:T(8,128)S(1)} custom-call(f32[4,512,128]{2,1,0:T(8,128)S(1)} %pad_maximum_fusion.refs_0_, bf16[2,520,128]{2,1,0:T(8,128)(2,1)S(1)} %get-tuple-element.5.refs_1_, bf16[4,2,520,128]{3,2,1,0:T(8,128)(2,1)S(1)} %collective-permute-done.2.refs_2_), custom_call_target="tpu_custom_call" | custom-call | flops 15728640 | bytes 4194304 | tf_op jit(solution)/shard_map/pallas_call | solution.py:178
  60.5 5.5 %shard_map.69.refs_1_ = f32[4,512,128]{2,1,0:T(8,128)S(1)} custom-call(f32[4,512,128]{2,1,0:T(8,128)S(1)} %pad_maximum_fusion.refs_0_, f32[4,512,128]{2,1,0:T(8,128)S(1)} %shard_map.68.refs_1_, bf16[4,520,128]{2,1,0:T(8,128)(2,1)S(1)} %collective-permute-done.3.refs_2_, bf16[4,520,128]{2,1,0:T(8,128)(2,1)S(1)} %collective-permute-done.4.refs_3_), custom_call_target="tpu_custom_call" | custom-call | flops 31457280 | bytes 4194304 | tf_op jit(solution)/shard_map/pallas_call | solution.py:178
  66.1 1.9 %collective-permute-done.5.refs_2_ = bf16[2,520,128]{2,1,0:T(8,128)(2,1)S(1)} collective-permute-done((bf16[2,520,128]{2,1,0:T(8,128)(2,1)S(1)}, bf16[2,520,128]{2,1,0:T(8,128)(2,1)S(1)}, u32[]{:S(2)}, u32[]{:S(2)}) %collective-permute-start.5) | collective-permute-done | bytes 266272 | tf_op jit(solution)/shard_map/ppermute | solution.py:30
  68.0 3.8 %collective-permute-done.6.refs_3_ = bf16[2,520,128]{2,1,0:T(8,128)(2,1)S(1)} collective-permute-done((bf16[2,520,128]{2,1,0:T(8,128)(2,1)S(1)}, bf16[2,520,128]{2,1,0:T(8,128)(2,1)S(1)}, u32[]{:S(2)}, u32[]{:S(2)}) %collective-permute-start.6) | collective-permute-done | bytes 266272 | tf_op jit(solution)/shard_map/ppermute | solution.py:30
  71.8 3.6 %shard_map.70 = f32[3,512,128]{2,1,0:T(8,128)S(1)} custom-call(f32[4,512,128]{2,1,0:T(8,128)S(1)} %pad_maximum_fusion.refs_0_, f32[4,512,128]{2,1,0:T(8,128)S(1)} %shard_map.69.refs_1_, bf16[2,520,128]{2,1,0:T(8,128)(2,1)S(1)} %collective-permute-done.5.refs_2_, bf16[2,520,128]{2,1,0:T(8,128)(2,1)S(1)} %collective-permute-done.6.refs_3_), custom_call_target="tpu_custom_call" | custom-call | flops 15728640 | bytes 4194304 | tf_op jit(solution)/shard_map/pallas_call | solution.py:178
  75.4 0.3 slice_reduce_fusion
  75.7 4.5 %collective-permute-start.8 = (f32[512]{0:T(512)S(1)}, f32[512]{0:T(512)S(1)}, u32[]{:S(2)}, u32[]{:S(2)}) collective-permute-start(f32[512]{0:T(512)S(1)} %get-tuple-element.9), channel_id=1, source_target_pairs={{8,0},{16,8},{24,16},{32,24},{40,32},{48,40},{56,48},{9,1},{17,9},... | collective-permute-start | bytes 6152 | tf_op jit(solution)/shard_map/ppermute | solution.py:36
  80.2 1.9 %collective-permute-start.7 = (f32[512]{0:T(512)S(1)}, f32[512]{0:T(512)S(1)}, u32[]{:S(2)}, u32[]{:S(2)}) collective-permute-start(f32[512]{0:T(512)S(1)} %get-tuple-element.8), channel_id=1, source_target_pairs={{0,8},{8,16},{16,24},{24,32},{32,40},{40,48},{48,56},{1,9},{9,17},... | collective-permute-start | bytes 6152 | tf_op jit(solution)/shard_map/ppermute | solution.py:36
  82.3 1.0 collective-permute-done.7
  83.4 0.3 fusion.1
  83.8 29.9 %all_to_all.10 = f32[64,2,8,128]{3,2,1,0:T(8,128)S(1)} all-to-all(f32[64,2,8,128]{3,2,1,0:T(8,128)S(1)} %pad_maximum_fusion.3), channel_id=1, replica_groups=mesh['y'=8,'zl'=4,'c'=2,'zh'=2,'x'=4] {'y','zh','x'}, dimensions={0} | all-to-all | bytes 1048576 | tf_op jit(solution)/shard_map/all_to_all | solution.py:252
  113.8 0.6 fusion.14
  (44 shorter events, 1.0 us)
Async XLA Ops:
  0.6 9.4 %copy-start.8 = (bf16[1,1,64,8]{2,3,1,0:T(8,128)(2,1)S(1)}, bf16[1,1,64,8]{2,3,1,0:T(8,128)(2,1)}, u32[]{:S(2)}) copy-start(bf16[1,1,64,8]{2,3,1,0:T(8,128)(2,1)} %param.8) | copy-start | bytes 3076
  0.6 9.6 %copy-start.1 = (s32[1,1,64,1]{2,3,1,0:T(1,128)S(1)}, s32[1,1,64,1]{2,3,1,0:T(1,128)}, u32[]{:S(2)}) copy-start(s32[1,1,64,1]{2,3,1,0:T(1,128)} %param.9) | copy-start | bytes 772
  0.7 9.6 %copy-start = (bf16[1,1,64,64,128]{4,3,2,1,0:T(8,128)(2,1)S(1)}, bf16[1,1,64,64,128]{4,3,2,1,0:T(8,128)(2,1)}, u32[]{:S(2)}) copy-start(bf16[1,1,64,64,128]{4,3,2,1,0:T(8,128)(2,1)} %param.7) | copy-start | bytes 3145732
  2.4 22.6 %all-to-all-start = ((f32[8,128,128]{2,1,0:T(8,128)}), f32[8,128,128]{2,1,0:T(8,128)S(1)}, u32[]{:S(2)}, u32[]{:S(2)}) async-start(f32[8,128,128]{2,1,0:T(8,128)} %broadcast_in_dim.18), calls=%async_computation | async-start | bytes 1048576 | tf_op jit(solution)/shard_map/all_to_all | solution.py:226
  12.7 26.5 %collective-permute-start.2 = (bf16[4,2,520,128]{3,2,1,0:T(8,128)(2,1)S(1)}, bf16[4,2,520,128]{3,2,1,0:T(8,128)(2,1)S(1)}, u32[]{:S(2)}, u32[]{:S(2)}) collective-permute-start(bf16[4,2,520,128]{3,2,1,0:T(8,128)(2,1)S(1)} %get-tuple-element.6), channel_id=1, source_target_pairs={{0,8},{8,0},{1,9},{9,1},{2,10},{10,2},{3,11},{11,3},{4,12},{12,4},... | collective-permute-start | bytes 3194888 | tf_op jit(solution)/shard_map/ppermute | solution.py:214
  25.7 13.5 %copy-start.2 = (bf16[2,520,128]{2,1,0:T(8,128)(2,1)S(1)}, bf16[2,520,128]{2,1,0:T(8,128)(2,1)}, u32[]{:S(2)}) copy-start(bf16[2,520,128]{2,1,0:T(8,128)(2,1)} %get-tuple-element.19) | copy-start | bytes 798724
  26.0 9.3 %collective-permute-start.1 = (f32[512]{0:T(512)S(1)}, f32[512]{0:T(512)S(1)}, u32[]{:S(2)}, u32[]{:S(2)}) collective-permute-start(f32[512]{0:T(512)S(1)} %get-tuple-element.11), channel_id=1, source_target_pairs={{0,8},{8,16},{16,24},{24,32},{32,40},{40,48},{48,56},{1,9},{9,17},... | collective-permute-start | bytes 6152 | tf_op jit(solution)/shard_map/ppermute | solution.py:36
  33.4 4.9 %collective-permute-start = (f32[512]{0:T(512)S(1)}, f32[512]{0:T(512)S(1)}, u32[]{:S(2)}, u32[]{:S(2)}) collective-permute-start(f32[512]{0:T(512)S(1)} %get-tuple-element.10), channel_id=1, source_target_pairs={{8,0},{16,8},{24,16},{32,24},{40,32},{48,40},{56,48},{9,1},{17,9},... | collective-permute-start | bytes 6152 | tf_op jit(solution)/shard_map/ppermute | solution.py:36
  39.3 8.9 %copy-start.7 = (bf16[1,520,128]{2,1,0:T(8,128)(2,1)S(1)}, bf16[1,520,128]{2,1,0:T(8,128)(2,1)}, u32[]{:S(2)}) copy-start(bf16[1,520,128]{2,1,0:T(8,128)(2,1)} %get-tuple-element.17) | copy-start | bytes 399364
  39.3 21.2 %collective-permute-start.3 = (bf16[4,520,128]{2,1,0:T(8,128)(2,1)S(1)}, bf16[4,520,128]{2,1,0:T(8,128)(2,1)S(1)}, u32[]{:S(2)}, u32[]{:S(2)}) collective-permute-start(bf16[4,520,128]{2,1,0:T(8,128)(2,1)S(1)} %pad_maximum_fusion.1), channel_id=1, source_target_pairs={{0,16},{4,20},{8,24},{12,28},{16,32},{20,36},{24,40},{28,44},{32,4... | collective-permute-start | bytes 1597448 | tf_op jit(solution)/shard_map/ppermute | solution.py:30
  43.4 7.5 %copy-start.6 = (bf16[1,520,128]{2,1,0:T(8,128)(2,1)S(1)}, bf16[1,520,128]{2,1,0:T(8,128)(2,1)}, u32[]{:S(2)}) copy-start(bf16[1,520,128]{2,1,0:T(8,128)(2,1)} %get-tuple-element.16) | copy-start | bytes 399364
  43.5 13.4 %copy-start.3 = (f32[512,1]{1,0:T(8,128)S(1)}, f32[512,1]{1,0:T(8,128)}, u32[]{:S(2)}) copy-start(f32[512,1]{1,0:T(8,128)} %copy.14) | copy-start | bytes 6148
  43.5 13.4 %copy-start.4 = (f32[512,1]{1,0:T(8,128)S(1)}, f32[512,1]{1,0:T(8,128)}, u32[]{:S(2)}) copy-start(f32[512,1]{1,0:T(8,128)} %copy.13) | copy-start | bytes 6148
  43.5 17.0 %collective-permute-start.4 = (bf16[4,520,128]{2,1,0:T(8,128)(2,1)S(1)}, bf16[4,520,128]{2,1,0:T(8,128)(2,1)S(1)}, u32[]{:S(2)}, u32[]{:S(2)}) collective-permute-start(bf16[4,520,128]{2,1,0:T(8,128)(2,1)S(1)} %pad_maximum_fusion.2), channel_id=1, source_target_pairs={{0,52},{4,48},{8,60},{12,56},{16,0},{20,4},{24,8},{28,12},{32,16},... | collective-permute-start | bytes 1597448 | tf_op jit(solution)/shard_map/ppermute | solution.py:30
  48.3 9.0 %copy-start.5 = (f32[8,64,128]{2,1,0:T(8,128)S(1)}, f32[8,64,128]{2,1,0:T(8,128)}, u32[]{:S(2)}) copy-start(f32[8,64,128]{2,1,0:T(8,128)} %get-tuple-element.28) | copy-start | bytes 786436
  48.3 19.7 %collective-permute-start.5 = (bf16[2,520,128]{2,1,0:T(8,128)(2,1)S(1)}, bf16[2,520,128]{2,1,0:T(8,128)(2,1)S(1)}, u32[]{:S(2)}, u32[]{:S(2)}) collective-permute-start(bf16[2,520,128]{2,1,0:T(8,128)(2,1)S(1)} %pad_maximum_fusion.4), channel_id=1, source_target_pairs={{0,32},{4,36},{8,40},{12,44},{16,48},{20,52},{24,56},{28,60},{32,4... | collective-permute-start | bytes 798728 | tf_op jit(solution)/shard_map/ppermute | solution.py:30
  51.0 20.7 %collective-permute-start.6 = (bf16[2,520,128]{2,1,0:T(8,128)(2,1)S(1)}, bf16[2,520,128]{2,1,0:T(8,128)(2,1)S(1)}, u32[]{:S(2)}, u32[]{:S(2)}) collective-permute-start(bf16[2,520,128]{2,1,0:T(8,128)(2,1)S(1)} %pad_maximum_fusion.5), channel_id=1, source_target_pairs={{0,36},{4,32},{8,44},{12,40},{16,52},{20,48},{24,60},{28,56},{32,0... | collective-permute-start | bytes 798728 | tf_op jit(solution)/shard_map/ppermute | solution.py:30
  75.7 6.5 %collective-permute-start.8 = (f32[512]{0:T(512)S(1)}, f32[512]{0:T(512)S(1)}, u32[]{:S(2)}, u32[]{:S(2)}) collective-permute-start(f32[512]{0:T(512)S(1)} %get-tuple-element.9), channel_id=1, source_target_pairs={{8,0},{16,8},{24,16},{32,24},{40,32},{48,40},{56,48},{9,1},{17,9},... | collective-permute-start | bytes 6152 | tf_op jit(solution)/shard_map/ppermute | solution.py:36
  80.2 3.1 %collective-permute-start.7 = (f32[512]{0:T(512)S(1)}, f32[512]{0:T(512)S(1)}, u32[]{:S(2)}, u32[]{:S(2)}) collective-permute-start(f32[512]{0:T(512)S(1)} %get-tuple-element.8), channel_id=1, source_target_pairs={{0,8},{8,16},{16,24},{24,32},{32,40},{40,48},{48,56},{1,9},{9,17},... | collective-permute-start | bytes 6152 | tf_op jit(solution)/shard_map/ppermute | solution.py:36
where the time goes:
time: 115 us; the launch traced here: 114 us
  starting transfers between devices  45.3 us (39%)
  blocking collectives  29.9 us (26%)
  waiting for transfers between devices  14.9 us (13%)
  Pallas kernels  14.7 us (13%)
  local copies, waits for them, and re-layouts  6.52 us (6%)
  other arithmetic  1.87 us (2%)
    all_to_all x1, blocking collectives, body(): lax.all_to_all(jnp.concatenate(parts, axis=1), ('y',) + IMG, split_axis=0...  29.9 us
    ppermute x4, starting transfers between devices, ring_shift(): return lax.ppermute(value, ('zl', 'c', 'zh'), pairs)  17.4 us
    ppermute x4, starting transfers between devices, column_shift(): return lax.ppermute(value, ('zl', 'c'), pairs)  15.7 us
    pallas_call x3, Pallas kernels, terms(): pl.pallas_call(lambda *refs: terms_kernel(scale, sums is not None, picks,...  12.3 us
    all_to_all x1, starting transfers between devices, body(): lax.all_to_all(copies, 'y', split_axis=0, concat_axis=0, tiled=True)  7.64 us
    all_to_all x1, waiting for transfers between devices, body(): lax.all_to_all(copies, 'y', split_axis=0, concat_axis=0, tiled=True)  6.19 us
    ppermute x4, waiting for transfers between devices, ring_shift(): return lax.ppermute(value, ('zl', 'c', 'zh'), pairs)  5.69 us
    ppermute x1, starting transfers between devices, body(): swapped = lax.ppermute(other, 'c', [(0, 1), (1, 0)])  4.62 us
  transfers between devices with their start and end apart: 10, of which 5 were waited for; matrix products, arithmetic and copies ran while one was open for 4% of the time, Pallas kernels for 10%

commit v1 on v0

v1 whole, which is shorter than its diff:
```python
import jax
import jax.numpy as jnp
from jax import lax
from jax.experimental import pallas as pl
from jax.experimental.pallas import tpu as pltpu
from jax.sharding import Mesh
from jax.sharding import PartitionSpec as P


SMOOTH = 0.0025
PARAMS = 8
STRIP = 16
ROWS, CLASSES, CORES, HALVES, DEPTH = 8, 4, 2, 2, 4
RING = CLASSES * HALVES
TILE = ("y", "zl", "c")
IMG = ("zh", "x")

SMEM = pl.BlockSpec(memory_space=pltpu.SMEM)
VMEM = pl.BlockSpec(memory_space=pltpu.VMEM)


def ring_shift(value, steps):
    pairs = []
    for low in range(CLASSES):
        for core in range(CORES):
            for high in range(HALVES):
                z = (high * CLASSES + low + steps) % RING
                source = (low * CORES + core) * HALVES + high
                pairs.append((source, ((z % CLASSES) * CORES + core) * HALVES + z // CLASSES))
    return lax.ppermute(value, ("zl", "c", "zh"), pairs)


def column_shift(value, steps):
    count = CLASSES * CORES
    pairs = [(k, k + steps) for k in range(count) if 0 <= k + steps < count]
    return lax.ppermute(value, ("zl", "c"), pairs)


def in_vmem(*arrays):
    return [pltpu.with_memory_space_constraint(a, pltpu.VMEM) for a in arrays]


def fill_table(dest_ref, table):
    def clear(index, carry):
        table[index] = -1
        return carry

    lax.fori_loop(0, table.shape[0], clear, 0, unroll=8)

    def note(index, carry):
        place = dest_ref[index] * 2
        second = (table[place] >= 0).astype(jnp.int32)
        table[place + second] = index
        return carry

    lax.fori_loop(0, dest_ref.shape[0], note, 0, unroll=4)


def pack_kernel(here_ref, dest_ref, params_ref, blocks_ref, near_ref, own_ref, other_ref, table, shifted, columns, rim, lines):
    number, tile_rows, tile_cols = blocks_ref.shape
    fill_table(dest_ref, table)
    for k in range(3):
        shifted[k] = params_ref[...] if k == 0 else pltpu.roll(params_ref[...], k * PARAMS, 1)

    lane8 = lax.broadcasted_iota(jnp.int32, (8, tile_cols), 1)
    sub8 = lax.broadcasted_iota(jnp.int32, (8, tile_cols), 0)
    pick = jnp.where(((sub8 == 0) & (lane8 == tile_cols - 1)) | ((sub8 == 1) & (lane8 == 0)), 1.0, 0.0).astype(jnp.bfloat16)
    flat = lax.dot_general(
        pick,
        blocks_ref[...].reshape(number * tile_rows, tile_cols),
        (((1,), (1,)), ((), ())),
        preferred_element_type=jnp.float32,
    )
    pairs = number // 2
    for m in range(pairs):
        part = slice(m * tile_cols, (m + 1) * tile_cols)
        columns[0, m : m + 1, :] = flat[0:1, part]
        columns[1, m : m + 1, :] = flat[1:2, part]
    left_half = lax.broadcasted_iota(jnp.int32, (pairs, tile_cols), 1) < tile_rows
    last, first = columns[0], columns[1]
    rim[0] = jnp.where(left_half, last, pltpu.roll(first, tile_rows, 1))
    rim[1] = jnp.where(left_half, pltpu.roll(last, tile_rows, 1), first)

    low, core = here_ref[0], here_ref[1]
    count = CLASSES * CORES
    west_half = lax.broadcasted_iota(jnp.int32, (1, tile_cols), 1) < tile_rows
    pixels = ROWS * tile_rows

    for kind in range(CORES):
        for d in range(CLASSES):
            column = ((low + d) % CLASSES) * CORES + (core + kind) % CORES
            unit = other_ref.at[d] if kind == 1 else near_ref if d == 0 else own_ref.at[d - 1]

            def place(row, carry):
                tile = row * count + column
                for slot in (0, 1):
                    block = table[2 * tile + slot]
                    west = jnp.where(column > 0, table[jnp.maximum(2 * tile - 2, 0) + slot], -1)
                    east = jnp.where(column < count - 1, table[jnp.minimum(2 * tile + 2, 2 * ROWS * count - 2) + slot], -1)
                    values = blocks_ref[jnp.maximum(block, 0)]
                    start = pl.multiple_of(row * tile_rows, tile_rows)
                    unit[slot, pl.ds(start, tile_rows), :] = jnp.where(block >= 0, values, jnp.zeros_like(values))
                    sides = []
                    line = jnp.zeros((1, tile_cols), jnp.float32)
                    for k, index in enumerate((block, west, east)):
                        safe = jnp.maximum(index, 0)
                        line = line + jnp.where(index >= 0, shifted[k, pl.ds(safe, 1), :], 0.0)
                        if k:
                            sides.append(jnp.where(index >= 0, rim[safe % 2, pl.ds(safe // 2, 1), :], 0.0))
                    lines[0, slot, pl.ds(row, 1), :] = jnp.where(west_half, sides[0], sides[1])
                    lines[1, slot, pl.ds(row, 1), :] = line
                return carry

            lax.fori_loop(0, ROWS, place, 0)
            for slot in (0, 1):
                for k in (0, 1):
                    unit[slot, pixels + k * ROWS : pixels + (k + 1) * ROWS, :] = lines[k, slot].astype(unit.dtype)


def pack(here, dest, params_wide, blocks):
    number, tile_rows, tile_cols = blocks.shape
    unit = (2, ROWS * tile_rows + 2 * ROWS, tile_cols)
    return pl.pallas_call(
        pack_kernel,
        out_shape=[pltpu.VMEM(lead + unit, jnp.bfloat16) for lead in ((), (CLASSES - 1,), (CLASSES,))],
        in_specs=[SMEM, SMEM, VMEM, VMEM],
        out_specs=[VMEM] * 3,
        scratch_shapes=[
            pltpu.SMEM((2 * ROWS * CLASSES * CORES,), jnp.int32),
            pltpu.VMEM((3,) + params_wide.shape, jnp.float32),
            pltpu.VMEM((2, number // 2, tile_cols), jnp.float32),
            pltpu.VMEM((2, number // 2, tile_cols), jnp.float32),
            pltpu.VMEM((2, 2, ROWS, tile_cols), jnp.float32),
        ],
        cost_estimate=pl.CostEstimate(flops=0, bytes_accessed=6 << 20, transcendentals=0),
        compiler_params=pltpu.CompilerParams(vmem_limit_bytes=8 << 20),
        name="pack",
    )(here, dest, *in_vmem(params_wide, blocks))


def turned(rows):
    size = rows.shape[1]
    return jnp.transpose(jnp.concatenate([rows, jnp.zeros((size - rows.shape[0], size), rows.dtype)]))


def maps_kernel(column_ref, got_ref, maps_ref, tall, side):
    tile_cols = got_ref.shape[2]
    tile_rows = (got_ref.shape[1] - ROWS) // 2
    pixels = ROWS * tile_rows
    column = column_ref[0]
    lane = lax.broadcasted_iota(jnp.int32, (tile_rows, tile_cols), 1)

    def finish(part, p, q, albedo):
        maps_ref[0, part, :] = p
        maps_ref[1, part, :] = q
        maps_ref[2, part, :] = 1.0 / jnp.sqrt(1.0 + p * p + q * q)
        maps_ref[3, part, :] = albedo

    for row in range(ROWS):
        tall[8 + row * tile_rows : 8 + (row + 1) * tile_rows, :] = got_ref[row, :tile_rows, :]
    tall[7:8, :] = got_ref[0, 0:1, :]
    tall[8 + pixels : 9 + pixels, :] = got_ref[ROWS - 1, tile_rows - 1 : tile_rows, :]
    beside, beyond, shade, mine = [
        jnp.concatenate([got_ref[row, 2 * tile_rows + k : 2 * tile_rows + k + 1, :] for row in range(ROWS)]) for k in range(4)
    ]
    side[...] = turned(beside)
    for row in range(ROWS):
        start = 8 + row * tile_rows
        height = tall[start : start + tile_rows, :]
        west = pltpu.roll(side[:tile_rows, :], (tile_cols - row) % tile_cols, 1)
        east = pltpu.roll(side[tile_rows:, :], tile_cols - 1 - row, 1)
        before = jnp.where(lane == 0, jnp.where(column == 0, height, west), pltpu.roll(height, 1, 1))
        after = jnp.where(
            lane == tile_cols - 1,
            jnp.where(column == CLASSES * CORES - 1, height, east),
            pltpu.roll(height, tile_cols - 1, 1),
        )
        p = (after - before) * 0.5
        q = (tall[start + 1 : start + 1 + tile_rows, :] - tall[start - 1 : start - 1 + tile_rows, :]) * 0.5
        finish(slice(row * tile_rows, (row + 1) * tile_rows), p, q, got_ref[row, tile_rows : 2 * tile_rows, :])

    lane = lax.broadcasted_iota(jnp.int32, (ROWS, tile_cols), 1)
    p = jnp.where(lane < tile_rows, mine - beyond, beyond - mine) * 0.5
    lower = jnp.concatenate([pltpu.roll(beside, tile_rows - 1, 1)[1:], beside[ROWS - 1 :]])
    upper = jnp.concatenate([beside[:1], pltpu.roll(beside, tile_cols - tile_rows + 1, 1)[:-1]])
    place = lane % tile_rows
    following = jnp.where(place == tile_rows - 1, lower, pltpu.roll(beside, tile_cols - 1, 1))
    preceding = jnp.where(place == 0, upper, pltpu.roll(beside, 1, 1))
    finish(slice(pixels, pixels + ROWS), p, (following - preceding) * 0.5, shade)


def make_maps(column, got):
    tile_cols = got.shape[2]
    pixels = ROWS * (got.shape[1] - ROWS) // 2
    return pl.pallas_call(
        maps_kernel,
        out_shape=pltpu.VMEM((4, pixels + ROWS, tile_cols), jnp.float32),
        in_specs=[SMEM, VMEM],
        out_specs=VMEM,
        scratch_shapes=[
            pltpu.VMEM((pixels + 16, tile_cols), jnp.float32),
            pltpu.VMEM((tile_cols, tile_cols), jnp.float32),
        ],
        cost_estimate=pl.CostEstimate(flops=0, bytes_accessed=3 << 20, transcendentals=0),
        compiler_params=pltpu.CompilerParams(vmem_limit_bytes=4 << 20),
        name="maps",
    )(column, *in_vmem(got))


def add_block(maps, totals, values, bright):
    pw, qw, w, albedo = maps
    sum_x, sum_y, sum_z, shade = totals
    sx, sy, sz, vx, vy, vz, mix, gain = values
    mix2 = mix * 2.0
    rest = 1.0 - mix
    bright = bright.astype(jnp.float32)
    ci = sz * w - sx * pw - sy * qw
    ce = vz * w - vx * pw - vy * qw
    square = ci * ci + SMOOTH
    inv_root = lax.rsqrt(square)
    mu = (ci + square * inv_root) * 0.5
    inv = 1.0 / (mu + ce)
    k = mix2 * inv
    u = mu * inv
    c = ce * inv
    shading = mu * (k + rest)
    misfit = (gain * albedo) * shading - bright
    scaled = gain * misfit
    shade = shade + scaled * shading
    gs = scaled * albedo
    gk = gs * k
    gl = gk * c + gs * rest
    gi = gl * (mu * inv_root)
    ge = gk * u
    return (
        sum_x + (gi * sx - ge * vx),
        sum_y + (gi * sy - ge * vy),
        sum_z + (gi * sz - ge * vz),
        shade,
    )


def terms_kernel(scale, with_sums, picks, *refs):
    column_ref, maps_ref, *refs = refs
    sums_ref = None
    if with_sums:
        sums_ref, *refs = refs
    got, refs = refs[: len(picks)], refs[len(picks) :]
    out_ref, lines, params, sem, *refs = refs
    units = [ref.at[pick] for ref, some in zip(got, picks) for pick in some]
    tile_cols = maps_ref.shape[2]
    pixels = maps_ref.shape[1] - ROWS
    tile_rows = pixels // ROWS
    for index, unit in enumerate(units):
        lines[index * ROWS : (index + 1) * ROWS, :] = unit[pixels + ROWS :, :].astype(jnp.float32)
    copy = pltpu.make_async_copy(lines, params, sem)
    copy.start()
    copy.wait()

    def run(part, size, values_of):
        p, q, w, albedo = (maps_ref[k, part, :] for k in range(4))
        if with_sums:
            totals = tuple(sums_ref[k, part, :] for k in range(4))
        else:
            totals = (jnp.zeros((size, tile_cols), jnp.float32),) * 4
        maps = (p * w, q * w, w, albedo)
        for number, unit in enumerate(units):
            totals = add_block(maps, totals, values_of(number), unit[part, :])
        if scale is None:
            for k, total in enumerate(totals):
                out_ref[k, part, :] = total
            return None
        sum_x, sum_y, sum_z, shade = totals
        up = (w * w * w) * (sum_z - p * sum_x - q * sum_y)
        half_x = (-(w * sum_x) - p * up) * (0.5 * scale)
        half_y = (-(w * sum_y) - q * up) * (0.5 * scale)
        return half_x, half_y, shade * scale

    def strip(index, carry):
        first = pl.multiple_of(index * STRIP, STRIP)
        row = index // (tile_rows // STRIP)
        result = run(pl.ds(first, STRIP), STRIP, lambda number: [params[number * ROWS + row, k] for k in range(PARAMS)])
        if result is not None:
            slope_x, slope_y, _ = refs
            slope_x[pl.ds(first, STRIP), :] = result[0]
            slope_y[pl.ds(pl.multiple_of(first + 8, 8), STRIP), :] = result[1]
            for half in range(STRIP // 8):
                out_ref[index * (STRIP // 8) + half, 8:16, :] = result[2][half * 8 : half * 8 + 8]
        return carry

    lax.fori_loop(0, pixels // STRIP, strip, 0)

    west_half = lax.broadcasted_iota(jnp.int32, (ROWS, tile_cols), 1) < tile_rows

    def side_values(number):
        rows = lines[number * ROWS : (number + 1) * ROWS, :]
        values = []
        for k in range(PARAMS):
            west, east = (
                jnp.broadcast_to(rows[:, n * PARAMS + k : n * PARAMS + k + 1], (ROWS, tile_cols)) for n in (1, 2)
            )
            values.append(jnp.where(west_half, west, east))
        return values

    result = run(slice(pixels, pixels + ROWS), ROWS, side_values)
    if result is None:
        return

    slope_x, slope_y, side = refs
    column = column_ref[0]
    side[...] = turned(result[0])
    slope_y[7:8, :] = -slope_y[8:9, :]
    slope_y[8 + pixels : 9 + pixels, :] = -slope_y[7 + pixels : 8 + pixels, :]
    lane = lax.broadcasted_iota(jnp.int32, (tile_rows, tile_cols), 1)
    for row in range(ROWS):
        start = row * tile_rows
        here = slope_x[start : start + tile_rows, :]
        west = pltpu.roll(side[:tile_rows, :], (tile_cols - row) % tile_cols, 1)
        east = pltpu.roll(side[tile_rows:, :], tile_cols - 1 - row, 1)
        before = jnp.where(lane == 0, jnp.where(column == 0, -here, west), pltpu.roll(here, 1, 1))
        after = jnp.where(
            lane == tile_cols - 1,
            jnp.where(column == CLASSES * CORES - 1, -here, east),
            pltpu.roll(here, tile_cols - 1, 1),
        )
        spread = before - after + slope_y[start + 7 : start + 7 + tile_rows, :] - slope_y[start + 9 : start + 9 + tile_rows, :]
        for group in range(tile_rows // 8):
            out_ref[row * (tile_rows // 8) + group, 0:8, :] = spread[group * 8 : group * 8 + 8]


def terms(column, maps, sums, got, scale):
    arrays, picks = zip(*got)
    count = sum(len(some) for some in picks)
    given = [maps] + ([] if sums is None else [sums]) + list(arrays)
    rows, cols = maps.shape[1:]
    scratch = [
        pltpu.VMEM((count * ROWS, cols), jnp.float32),
        pltpu.SMEM((count * ROWS, cols), jnp.float32),
        pltpu.SemaphoreType.DMA,
    ]
    if scale is None:
        out = (4, rows, cols)
    else:
        out = ((rows - ROWS) // 8, 16, cols)
        scratch += [pltpu.VMEM((rows - ROWS, cols), jnp.float32), pltpu.VMEM((rows - ROWS + 16, cols), jnp.float32)]
        scratch += [pltpu.VMEM((cols, cols), jnp.float32)]
    return pl.pallas_call(
        lambda *refs: terms_kernel(scale, sums is not None, picks, *refs),
        out_shape=pltpu.VMEM(out, jnp.float32),
        in_specs=[SMEM] + [VMEM] * len(given),
        out_specs=VMEM,
        scratch_shapes=scratch,
        cost_estimate=pl.CostEstimate(flops=60 * count * rows * cols, bytes_accessed=4 << 20, transcendentals=0),
        compiler_params=pltpu.CompilerParams(vmem_limit_bytes=4 << 20),
    )(column, *in_vmem(*given))


EACH2 = [(0,), (1,)]
EACH4 = EACH2 + [(2,), (3,)]


def body(heights, albedo, blocks, block_params, block_dest):
    column_here = lax.axis_index(("zl", "c"))
    tile_rows, tile_cols = heights.shape[1:]
    block_count = block_dest.shape[2]

    params_wide = jnp.pad(
        block_params.reshape(block_count, PARAMS).astype(jnp.float32), ((0, 0), (0, tile_cols - PARAMS))
    )
    here = jnp.stack([lax.axis_index("zl"), lax.axis_index("c")]).astype(jnp.int32)
    near, own, other = pack(
        here,
        block_dest.reshape(block_count),
        params_wide,
        blocks.reshape(block_count, tile_rows, tile_cols),
    )
    swapped = lax.ppermute(other, "c", [(0, 1), (1, 0)])
    to_right = jnp.concatenate([own[0], swapped[1]])
    to_left = jnp.concatenate([own[2], swapped[3]])
    to_right2 = jnp.stack([own[1, 0], swapped[2, 0]])
    to_left2 = jnp.stack([own[1, 1], swapped[2, 1]])
    right = ring_shift(to_right, 1)
    left = ring_shift(to_left, -1)
    right2 = ring_shift(to_right2, 2)
    left2 = ring_shift(to_left2, -2)

    height, shade = heights[0], albedo[0]
    first, last = jnp.stack([height[:, 0], height[:, 1], shade[:, 0]]), jnp.stack([height[:, -1], height[:, -2], shade[:, -1]])
    from_west = column_shift(last, 1)
    from_east = column_shift(first, -1)
    beside = jnp.concatenate([from_west, from_east], axis=1)
    mine = jnp.concatenate([first[:1], last[:1]], axis=1)
    rows = jnp.concatenate([beside, mine, jnp.zeros((ROWS - 4, tile_cols), jnp.float32)])
    copies = jnp.broadcast_to(jnp.concatenate([height, shade, rows])[None], (ROWS, 2 * tile_rows + ROWS, tile_cols))
    gathered = lax.all_to_all(copies, "y", split_axis=0, concat_axis=0, tiled=True)
    column = column_here.reshape(1).astype(jnp.int32)
    maps = make_maps(column, gathered)

    sums = terms(column, maps, None, [(near, [(0,), (1,)]), (swapped, [(0, 0), (0, 1)])], None)
    sums = terms(column, maps, sums, [(right, EACH4), (left, EACH4)], None)
    parts = terms(column, maps, sums, [(right2, EACH2), (left2, EACH2)], 1.0 / block_count)
    summed = jnp.sum(lax.all_to_all(parts, ("y",) + IMG, split_axis=0, concat_axis=0, tiled=True), axis=0)
    half = tile_rows // (HALVES * DEPTH)
    return (summed[None, :half], summed[None, half:])


def solution(mesh):
    physical = Mesh(mesh.devices.reshape(ROWS, CLASSES, CORES, HALVES, DEPTH), TILE + IMG)
    placed = (
        P(TILE, None, None),
        P(TILE, None, None),
        P(TILE, IMG, None, None, None),
        P(TILE, IMG, None, None),
        P(TILE, IMG, None, None),
    )

    return jax.shard_map(
        body,
        mesh=physical,
        in_specs=placed,
        out_specs=(P(TILE, IMG, None), P(TILE, IMG, None)),
        check_vma=False,
    )
```

time: 115 us -> 105 us (0.913)
  the two profiles are of different devices: /device:TPU:1 before, /device:TPU:6 now
where the time goes in v1:
time: 105 us; the launch traced here: 104 us
  blocking collectives  35 us (33%)
  starting transfers between devices  33.5 us (32%)
  Pallas kernels  18.1 us (17%)
  waiting for transfers between devices  7.71 us (7%)
  local copies, waits for them, and re-layouts  5.39 us (5%)
  other arithmetic  3.49 us (3%)
    all_to_all x1, blocking collectives, body(): lax.all_to_all(parts, ('y',) + IMG, split_axis=0, concat_axis=0, tiled=True)  35 us
    ppermute x4, starting transfers between devices, ring_shift(): return lax.ppermute(value, ('zl', 'c', 'zh'), pairs)  20.8 us
    pallas_call x3, Pallas kernels, terms(): pl.pallas_call(lambda *refs: terms_kernel(scale, sums is not None, picks,...  13.5 us
    all_to_all x1, starting transfers between devices, body(): lax.all_to_all(copies, 'y', split_axis=0, concat_axis=0, tiled=True)  7.1 us
    ppermute x4, waiting for transfers between devices, ring_shift(): return lax.ppermute(value, ('zl', 'c', 'zh'), pairs)  5.32 us
    pallas_call x1, Pallas kernels, pack(): pl.pallas_call(pack_kernel, out_shape=[pltpu.VMEM(lead + unit, jnp.bfloat...  4.18 us
    ppermute x2, starting transfers between devices, column_shift(): return lax.ppermute(value, ('zl', 'c'), pairs)  3.69 us
    unnamed x13, local copies, waits for them, and re-layouts  2.68 us
  transfers between devices with their start and end apart: 8, of which 2 were waited for; matrix products, arithmetic and copies ran while one was open for 5% of the time, Pallas kernels for 9%

profile of v1, /device:TPU:6, one launch (start us, length us, event | category | flops | bytes accessed | tf_op | source)
XLA Modules:
  0.0 104.1 jit_solution(249736877325680016)
XLA Ops:
  0.7 0.8 copy.8
  1.4 0.1 pad_add_fusion.here_ref
  1.5 1.2 %copy-done = bf16[1,1,64,64,128]{4,3,2,1,0:T(8,128)(2,1)S(1)} copy-done((bf16[1,1,64,64,128]{4,3,2,1,0:T(8,128)(2,1)S(1)}, bf16[1,1,64,64,128]{4,3,2,1,0:T(8,128)(2,1)}, u32[]{:S(2)}) %copy-start) | copy-done | bytes 1048600
  2.8 0.7 copy-done.1
  3.4 4.2 %pack.1 = (bf16[2,528,128]{2,1,0:T(8,128)(2,1)S(1)}, bf16[3,2,528,128]{3,2,1,0:T(8,128)(2,1)S(1)}, bf16[4,2,528,128]{3,2,1,0:T(8,128)(2,1)S(1)}) custom-call(s32[2]{0:T(128)S(1)} %pad_add_fusion.here_ref, s32[64]{0:T(128)S(1)} %bitcast.35, f32[64,128]{1,0:T(8,128)S(1)} %pad_convert_fusion.params_ref, bf16[64,64,128]{2,1,0:T(8,128)(2,1)S(1)} %bitcast.34), custom_call_target="tpu_custom_call" | custom-call | bytes 6291456 | tf_op jit(solution)/shard_map/pack/pallas_call | solution.py:123
  7.6 1.9 %collective-permute-start.2 = (bf16[4,2,528,128]{3,2,1,0:T(8,128)(2,1)S(1)}, bf16[4,2,528,128]{3,2,1,0:T(8,128)(2,1)S(1)}, u32[]{:S(2)}, u32[]{:S(2)}) collective-permute-start(bf16[4,2,528,128]{3,2,1,0:T(8,128)(2,1)S(1)} %get-tuple-element.6), channel_id=1, source_target_pairs={{0,8},{8,0},{1,9},{9,1},{2,10},{10,2},{3,11},{11,3},{4,12},{12,4},... | collective-permute-start | bytes 3244040 | tf_op jit(solution)/shard_map/ppermute | solution.py:377
  9.5 0.2 slice_reduce_fusion.3
  9.7 0.2 slice_reduce_fusion.5
  10.0 2.4 %collective-permute-start = (f32[3,64]{1,0:T(4,128)S(1)}, f32[3,64]{1,0:T(4,128)S(1)}, u32[]{:S(2)}, u32[]{:S(2)}) collective-permute-start(f32[3,64]{1,0:T(4,128)S(1)} %pad_maximum_fusion.4), channel_id=1, source_target_pairs={{0,8},{8,16},{16,24},{24,32},{32,40},{40,48},{48,56},{1,9},{9,17},... | collective-permute-start | bytes 2312 | tf_op jit(solution)/shard_map/ppermute | solution.py:36
  12.4 1.3 %collective-permute-start.1 = (f32[3,64]{1,0:T(4,128)S(1)}, f32[3,64]{1,0:T(4,128)S(1)}, u32[]{:S(2)}, u32[]{:S(2)}) collective-permute-start(f32[3,64]{1,0:T(4,128)S(1)} %pad_maximum_fusion.5), channel_id=1, source_target_pairs={{8,0},{16,8},{24,16},{32,24},{40,32},{48,40},{56,48},{9,1},{17,9},... | collective-permute-start | bytes 2312 | tf_op jit(solution)/shard_map/ppermute | solution.py:36
  13.7 0.8 slice_bitcast_fusion.6
  14.5 0.1 pad_maximum_fusion.7
  14.6 2.4 %collective-permute-done.1 = f32[3,64]{1,0:T(4,128)S(1)} collective-permute-done((f32[3,64]{1,0:T(4,128)S(1)}, f32[3,64]{1,0:T(4,128)S(1)}, u32[]{:S(2)}, u32[]{:S(2)}) %collective-permute-start.1) | collective-permute-done | bytes 800 | tf_op jit(solution)/shard_map/ppermute | solution.py:36
  16.9 0.1 pad_maximum_fusion.6
  17.0 0.8 broadcast_in_dim.16
  17.9 7.1 %all-to-all-start = ((f32[8,136,128]{2,1,0:T(8,128)}), f32[8,136,128]{2,1,0:T(8,128)S(1)}, u32[]{:S(2)}, u32[]{:S(2)}) async-start(f32[8,136,128]{2,1,0:T(8,128)} %broadcast_in_dim.16), calls=%async_computation | async-start | bytes 1114112 | tf_op jit(solution)/shard_map/all_to_all | solution.py:395
  25.0 0.8 pad_maximum_fusion
  25.9 4.4 %collective-permute-start.3 = (bf16[4,528,128]{2,1,0:T(8,128)(2,1)}, bf16[4,528,128]{2,1,0:T(8,128)(2,1)S(1)}, u32[]{:S(2)}, u32[]{:S(2)}) collective-permute-start(bf16[4,528,128]{2,1,0:T(8,128)(2,1)} %pad_maximum_fusion), channel_id=1, source_target_pairs={{0,16},{4,20},{8,24},{12,28},{16,32},{20,36},{24,40},{28,44},{32,4... | collective-permute-start | bytes 1622024 | tf_op jit(solution)/shard_map/ppermute | solution.py:30
  30.3 0.9 pad_maximum_fusion.1
  31.2 8.5 %collective-permute-start.4 = (bf16[4,528,128]{2,1,0:T(8,128)(2,1)}, bf16[4,528,128]{2,1,0:T(8,128)(2,1)S(1)}, u32[]{:S(2)}, u32[]{:S(2)}) collective-permute-start(bf16[4,528,128]{2,1,0:T(8,128)(2,1)} %pad_maximum_fusion.1), channel_id=1, source_target_pairs={{0,52},{4,48},{8,60},{12,56},{16,0},{20,4},{24,8},{28,12},{32,16},... | collective-permute-start | bytes 1622024 | tf_op jit(solution)/shard_map/ppermute | solution.py:30
  39.7 0.7 pad_maximum_fusion.2
  40.4 1.9 %collective-permute-start.5 = (bf16[2,528,128]{2,1,0:T(8,128)(2,1)}, bf16[2,528,128]{2,1,0:T(8,128)(2,1)S(1)}, u32[]{:S(2)}, u32[]{:S(2)}) collective-permute-start(bf16[2,528,128]{2,1,0:T(8,128)(2,1)} %pad_maximum_fusion.2), channel_id=1, source_target_pairs={{0,32},{4,36},{8,40},{12,44},{16,48},{20,52},{24,56},{28,60},{32,4... | collective-permute-start | bytes 811016 | tf_op jit(solution)/shard_map/ppermute | solution.py:30
  42.3 0.7 pad_maximum_fusion.3
  43.1 6.0 %collective-permute-start.6 = (bf16[2,528,128]{2,1,0:T(8,128)(2,1)}, bf16[2,528,128]{2,1,0:T(8,128)(2,1)S(1)}, u32[]{:S(2)}, u32[]{:S(2)}) collective-permute-start(bf16[2,528,128]{2,1,0:T(8,128)(2,1)} %pad_maximum_fusion.3), channel_id=1, source_target_pairs={{0,36},{4,32},{8,44},{12,40},{16,52},{20,48},{24,60},{28,56},{32,0... | collective-permute-start | bytes 811016 | tf_op jit(solution)/shard_map/ppermute | solution.py:30
  49.1 0.4 maps.1.refs_1_
  49.5 3.4 %shard_map.68.refs_2_ = f32[4,520,128]{2,1,0:T(8,128)S(1)} custom-call(s32[1]{0:T(128)} %bitcast.column_ref.refs_0_, f32[4,520,128]{2,1,0:T(8,128)S(1)} %maps.1.refs_1_, bf16[2,528,128]{2,1,0:T(8,128)(2,1)S(1)} %get-tuple-element.5.refs_2_, bf16[4,2,528,128]{3,2,1,0:T(8,128)(2,1)S(1)} %collective-permute-done.2.refs_3_), custom_call_target="tpu_custom_call" | custom-call | flops 15974400 | bytes 4194304 | tf_op jit(solution)/shard_map/pallas_call | solution.py:347
  52.9 5.3 %collective-permute-done.4.refs_4_ = bf16[4,528,128]{2,1,0:T(8,128)(2,1)S(1)} collective-permute-done((bf16[4,528,128]{2,1,0:T(8,128)(2,1)}, bf16[4,528,128]{2,1,0:T(8,128)(2,1)S(1)}, u32[]{:S(2)}, u32[]{:S(2)}) %collective-permute-start.4) | collective-permute-done | bytes 540704 | tf_op jit(solution)/shard_map/ppermute | solution.py:30
  58.2 5.8 %shard_map.69.refs_2_ = f32[4,520,128]{2,1,0:T(8,128)S(1)} custom-call(s32[1]{0:T(128)} %bitcast.column_ref.refs_0_, f32[4,520,128]{2,1,0:T(8,128)S(1)} %maps.1.refs_1_, f32[4,520,128]{2,1,0:T(8,128)S(1)} %shard_map.68.refs_2_, bf16[4,528,128]{2,1,0:T(8,128)(2,1)S(1)} %collective-permute-done.3.refs_3_, bf16[4,528,128]{2,1,0:T(8,128)(2,1)S(1)} %collective-permute-done.4.refs_4_), custom_call_target="tpu_custom_call" | custom-call | flops 31948800 | bytes 4194304 | tf_op jit(solution)/shard_map/pallas_call | solution.py:347
  64.1 4.3 %shard_map.70 = f32[64,16,128]{2,1,0:T(8,128)S(1)} custom-call(s32[1]{0:T(128)} %bitcast.column_ref.refs_0_, f32[4,520,128]{2,1,0:T(8,128)S(1)} %maps.1.refs_1_, f32[4,520,128]{2,1,0:T(8,128)S(1)} %shard_map.69.refs_2_, bf16[2,528,128]{2,1,0:T(8,128)(2,1)S(1)} %collective-permute-done.5.refs_3_, bf16[2,528,128]{2,1,0:T(8,128)(2,1)S(1)} %collective-permute-done.6.refs_4_), custom_call_target="tpu_custom_call" | custom-call | flops 15974400 | bytes 4194304 | tf_op jit(solution)/shard_map/pallas_call | solution.py:347
  68.4 35.0 %all_to_all.10 = f32[64,16,128]{2,1,0:T(8,128)S(1)} all-to-all(f32[64,16,128]{2,1,0:T(8,128)S(1)} %shard_map.70), channel_id=1, replica_groups=mesh['y'=8,'zl'=4,'c'=2,'zh'=2,'x'=4] {'y','zh','x'}, dimensions={0} | all-to-all | bytes 1048576 | tf_op jit(solution)/shard_map/all_to_all | solution.py:402
  103.4 0.1 reduce_sum.9
  103.5 0.6 slice_bitcast_fusion.8
  (24 shorter events, 0.2 us)
Async XLA Ops:
  0.6 8.9 %copy-start.5 = (f32[1,64,128]{2,1,0:T(8,128)S(1)}, f32[1,64,128]{2,1,0:T(8,128)}, u32[]{:S(2)}) copy-start(f32[1,64,128]{2,1,0:T(8,128)} %param.6) | copy-start | bytes 98308
  0.6 9.1 %copy-start.2 = (f32[1,64,128]{2,1,0:T(8,128)S(1)}, f32[1,64,128]{2,1,0:T(8,128)}, u32[]{:S(2)}) copy-start(f32[1,64,128]{2,1,0:T(8,128)} %param.5) | copy-start | bytes 98308
  1.5 1.2 %copy-start = (bf16[1,1,64,64,128]{4,3,2,1,0:T(8,128)(2,1)S(1)}, bf16[1,1,64,64,128]{4,3,2,1,0:T(8,128)(2,1)}, u32[]{:S(2)}) copy-start(bf16[1,1,64,64,128]{4,3,2,1,0:T(8,128)(2,1)} %param.7) | copy-start | bytes 3145732
  2.7 0.7 copy-start.1
  7.6 17.4 %collective-permute-start.2 = (bf16[4,2,528,128]{3,2,1,0:T(8,128)(2,1)S(1)}, bf16[4,2,528,128]{3,2,1,0:T(8,128)(2,1)S(1)}, u32[]{:S(2)}, u32[]{:S(2)}) collective-permute-start(bf16[4,2,528,128]{3,2,1,0:T(8,128)(2,1)S(1)} %get-tuple-element.6), channel_id=1, source_target_pairs={{0,8},{8,0},{1,9},{9,1},{2,10},{10,2},{3,11},{11,3},{4,12},{12,4},... | collective-permute-start | bytes 3244040 | tf_op jit(solution)/shard_map/ppermute | solution.py:377
  10.0 4.6 %collective-permute-start = (f32[3,64]{1,0:T(4,128)S(1)}, f32[3,64]{1,0:T(4,128)S(1)}, u32[]{:S(2)}, u32[]{:S(2)}) collective-permute-start(f32[3,64]{1,0:T(4,128)S(1)} %pad_maximum_fusion.4), channel_id=1, source_target_pairs={{0,8},{8,16},{16,24},{24,32},{32,40},{40,48},{48,56},{1,9},{9,17},... | collective-permute-start | bytes 2312 | tf_op jit(solution)/shard_map/ppermute | solution.py:36
  12.4 4.6 %collective-permute-start.1 = (f32[3,64]{1,0:T(4,128)S(1)}, f32[3,64]{1,0:T(4,128)S(1)}, u32[]{:S(2)}, u32[]{:S(2)}) collective-permute-start(f32[3,64]{1,0:T(4,128)S(1)} %pad_maximum_fusion.5), channel_id=1, source_target_pairs={{8,0},{16,8},{24,16},{32,24},{40,32},{48,40},{56,48},{9,1},{17,9},... | collective-permute-start | bytes 2312 | tf_op jit(solution)/shard_map/ppermute | solution.py:36
  17.9 31.2 %all-to-all-start = ((f32[8,136,128]{2,1,0:T(8,128)}), f32[8,136,128]{2,1,0:T(8,128)S(1)}, u32[]{:S(2)}, u32[]{:S(2)}) async-start(f32[8,136,128]{2,1,0:T(8,128)} %broadcast_in_dim.16), calls=%async_computation | async-start | bytes 1114112 | tf_op jit(solution)/shard_map/all_to_all | solution.py:395
  25.9 13.8 %copy-start.4 = (bf16[1,528,128]{2,1,0:T(8,128)(2,1)S(1)}, bf16[1,528,128]{2,1,0:T(8,128)(2,1)}, u32[]{:S(2)}) copy-start(bf16[1,528,128]{2,1,0:T(8,128)(2,1)} %get-tuple-element.19) | copy-start | bytes 405508
  25.9 27.0 %collective-permute-start.3 = (bf16[4,528,128]{2,1,0:T(8,128)(2,1)}, bf16[4,528,128]{2,1,0:T(8,128)(2,1)S(1)}, u32[]{:S(2)}, u32[]{:S(2)}) collective-permute-start(bf16[4,528,128]{2,1,0:T(8,128)(2,1)} %pad_maximum_fusion), channel_id=1, source_target_pairs={{0,16},{4,20},{8,24},{12,28},{16,32},{20,36},{24,40},{28,44},{32,4... | collective-permute-start | bytes 1622024 | tf_op jit(solution)/shard_map/ppermute | solution.py:30
  30.3 12.0 %copy-start.3 = (bf16[1,528,128]{2,1,0:T(8,128)(2,1)S(1)}, bf16[1,528,128]{2,1,0:T(8,128)(2,1)}, u32[]{:S(2)}) copy-start(bf16[1,528,128]{2,1,0:T(8,128)(2,1)} %get-tuple-element.18) | copy-start | bytes 405508
  31.2 27.1 %collective-permute-start.4 = (bf16[4,528,128]{2,1,0:T(8,128)(2,1)}, bf16[4,528,128]{2,1,0:T(8,128)(2,1)S(1)}, u32[]{:S(2)}, u32[]{:S(2)}) collective-permute-start(bf16[4,528,128]{2,1,0:T(8,128)(2,1)} %pad_maximum_fusion.1), channel_id=1, source_target_pairs={{0,52},{4,48},{8,60},{12,56},{16,0},{20,4},{24,8},{28,12},{32,16},... | collective-permute-start | bytes 1622024 | tf_op jit(solution)/shard_map/ppermute | solution.py:30
  40.4 23.7 %collective-permute-start.5 = (bf16[2,528,128]{2,1,0:T(8,128)(2,1)}, bf16[2,528,128]{2,1,0:T(8,128)(2,1)S(1)}, u32[]{:S(2)}, u32[]{:S(2)}) collective-permute-start(bf16[2,528,128]{2,1,0:T(8,128)(2,1)} %pad_maximum_fusion.2), channel_id=1, source_target_pairs={{0,32},{4,36},{8,40},{12,44},{16,48},{20,52},{24,56},{28,60},{32,4... | collective-permute-start | bytes 811016 | tf_op jit(solution)/shard_map/ppermute | solution.py:30
  43.1 21.0 %collective-permute-start.6 = (bf16[2,528,128]{2,1,0:T(8,128)(2,1)}, bf16[2,528,128]{2,1,0:T(8,128)(2,1)S(1)}, u32[]{:S(2)}, u32[]{:S(2)}) collective-permute-start(bf16[2,528,128]{2,1,0:T(8,128)(2,1)} %pad_maximum_fusion.3), channel_id=1, source_target_pairs={{0,36},{4,32},{8,44},{12,40},{16,52},{20,48},{24,60},{28,56},{32,0... | collective-permute-start | bytes 811016 | tf_op jit(solution)/shard_map/ppermute | solution.py:30

commit v2 on v1

--- a/solution.py
+++ b/solution.py
@@ -56,11 +56,20 @@
     lax.fori_loop(0, dest_ref.shape[0], note, 0, unroll=4)
 
 
-def pack_kernel(here_ref, dest_ref, params_ref, blocks_ref, near_ref, own_ref, other_ref, table, shifted, columns, rim, lines):
+def pack_kernel(
+    here_ref, dest_ref, params_ref, blocks_hbm, near_ref, right_ref, left_ref, right2_ref, left2_ref, other_ref,
+    blocks_ref, sem, table, shifted, columns, rim, lines,
+):
     number, tile_rows, tile_cols = blocks_ref.shape
+    fetch = pltpu.make_async_copy(blocks_hbm, blocks_ref, sem)
+    fetch.start()
     fill_table(dest_ref, table)
+    upright = params_ref[...].astype(jnp.float32)
+    upright = jnp.concatenate([upright, jnp.zeros((PARAMS, tile_cols - number), jnp.float32)], axis=1)
+    plain = turned(upright)[:number]
     for k in range(3):
-        shifted[k] = params_ref[...] if k == 0 else pltpu.roll(params_ref[...], k * PARAMS, 1)
+        shifted[k] = plain if k == 0 else pltpu.roll(plain, k * PARAMS, 1)
+    fetch.wait()
 
     lane8 = lax.broadcasted_iota(jnp.int32, (8, tile_cols), 1)
     sub8 = lax.broadcasted_iota(jnp.int32, (8, tile_cols), 0)
@@ -85,49 +94,62 @@
     count = CLASSES * CORES
     west_half = lax.broadcasted_iota(jnp.int32, (1, tile_cols), 1) < tile_rows
     pixels = ROWS * tile_rows
+    mine = {
+        0: (near_ref.at[0], near_ref.at[1]),
+        1: (right_ref.at[0], right_ref.at[1]),
+        2: (right2_ref.at[0], left2_ref.at[0]),
+        3: (left_ref.at[0], left_ref.at[1]),
+    }
 
     for kind in range(CORES):
         for d in range(CLASSES):
             column = ((low + d) % CLASSES) * CORES + (core + kind) % CORES
-            unit = other_ref.at[d] if kind == 1 else near_ref if d == 0 else own_ref.at[d - 1]
-
-            def place(row, carry):
-                tile = row * count + column
-                for slot in (0, 1):
-                    block = table[2 * tile + slot]
-                    west = jnp.where(column > 0, table[jnp.maximum(2 * tile - 2, 0) + slot], -1)
-                    east = jnp.where(column < count - 1, table[jnp.minimum(2 * tile + 2, 2 * ROWS * count - 2) + slot], -1)
-                    values = blocks_ref[jnp.maximum(block, 0)]
+            units = (other_ref.at[d, 0], other_ref.at[d, 1]) if kind else mine[d]
+
+            def place(step, carry):
+                found = []
+                for row in (step * 2, step * 2 + 1):
+                    tile = row * count + column
+                    for slot in (0, 1):
+                        block = table[2 * tile + slot]
+                        west = jnp.where(column > 0, table[jnp.maximum(2 * tile - 2, 0) + slot], -1)
+                        east = jnp.where(column < count - 1, table[jnp.minimum(2 * tile + 2, 2 * ROWS * count - 2) + slot], -1)
+                        values = blocks_ref[jnp.maximum(block, 0)]
+                        values = jnp.where(block >= 0, values, jnp.zeros_like(values))
+                        sides = []
+                        line = jnp.zeros((1, tile_cols), jnp.float32)
+                        for k, index in enumerate((block, west, east)):
+                            safe = jnp.maximum(index, 0)
+                            line = line + jnp.where(index >= 0, shifted[k, pl.ds(safe, 1), :], 0.0)
+                            if k:
+                                sides.append(jnp.where(index >= 0, rim[safe % 2, pl.ds(safe // 2, 1), :], 0.0))
+                        found.append((row, slot, values, jnp.where(west_half, sides[0], sides[1]), line))
+                for row, slot, values, side, line in found:
                     start = pl.multiple_of(row * tile_rows, tile_rows)
-                    unit[slot, pl.ds(start, tile_rows), :] = jnp.where(block >= 0, values, jnp.zeros_like(values))
-                    sides = []
-                    line = jnp.zeros((1, tile_cols), jnp.float32)
-                    for k, index in enumerate((block, west, east)):
-                        safe = jnp.maximum(index, 0)
-                        line = line + jnp.where(index >= 0, shifted[k, pl.ds(safe, 1), :], 0.0)
-                        if k:
-                            sides.append(jnp.where(index >= 0, rim[safe % 2, pl.ds(safe // 2, 1), :], 0.0))
-                    lines[0, slot, pl.ds(row, 1), :] = jnp.where(west_half, sides[0], sides[1])
+                    units[slot][pl.ds(start, tile_rows), :] = values
+                    lines[0, slot, pl.ds(row, 1), :] = side
                     lines[1, slot, pl.ds(row, 1), :] = line
                 return carry
 
-            lax.fori_loop(0, ROWS, place, 0)
+            lax.fori_loop(0, ROWS // 2, place, 0)
             for slot in (0, 1):
                 for k in (0, 1):
-                    unit[slot, pixels + k * ROWS : pixels + (k + 1) * ROWS, :] = lines[k, slot].astype(unit.dtype)
-
-
-def pack(here, dest, params_wide, blocks):
+                    units[slot][pixels + k * ROWS : pixels + (k + 1) * ROWS, :] = lines[k, slot].astype(jnp.bfloat16)
+
+
+def pack(here, dest, params, blocks):
     number, tile_rows, tile_cols = blocks.shape
-    unit = (2, ROWS * tile_rows + 2 * ROWS, tile_cols)
+    unit = (ROWS * tile_rows + 2 * ROWS, tile_cols)
     return pl.pallas_call(
         pack_kernel,
-        out_shape=[pltpu.VMEM(lead + unit, jnp.bfloat16) for lead in ((), (CLASSES - 1,), (CLASSES,))],
-        in_specs=[SMEM, SMEM, VMEM, VMEM],
-        out_specs=[VMEM] * 3,
+        out_shape=[pltpu.VMEM(lead + unit, jnp.bfloat16) for lead in ((2,), (2,), (2,), (1,), (1,), (CLASSES, 2))],
+        in_specs=[SMEM, SMEM, VMEM, pl.BlockSpec(memory_space=pltpu.HBM)],
+        out_specs=[VMEM] * 6,
         scratch_shapes=[
+            pltpu.VMEM(blocks.shape, jnp.bfloat16),
+            pltpu.SemaphoreType.DMA,
             pltpu.SMEM((2 * ROWS * CLASSES * CORES,), jnp.int32),
-            pltpu.VMEM((3,) + params_wide.shape, jnp.float32),
+            pltpu.VMEM((3, number, tile_cols), jnp.float32),
             pltpu.VMEM((2, number // 2, tile_cols), jnp.float32),
             pltpu.VMEM((2, number // 2, tile_cols), jnp.float32),
             pltpu.VMEM((2, 2, ROWS, tile_cols), jnp.float32),
@@ -135,7 +157,29 @@
         cost_estimate=pl.CostEstimate(flops=0, bytes_accessed=6 << 20, transcendentals=0),
         compiler_params=pltpu.CompilerParams(vmem_limit_bytes=8 << 20),
         name="pack",
-    )(here, dest, *in_vmem(params_wide, blocks))
+    )(here, *[pltpu.with_memory_space_constraint(a, pltpu.HBM) for a in (dest, params, blocks)])
+
+
+def join_kernel(swapped_ref, *refs):
+    own, (right_ref, left_ref, right2_ref, left2_ref) = refs[:4], refs[4:]
+    for half, some in zip((right_ref, left_ref, right2_ref, left2_ref), own):
+        half[: some.shape[0]] = some[...]
+    right_ref[2:4] = swapped_ref[1]
+    left_ref[2:4] = swapped_ref[3]
+    right2_ref[1] = swapped_ref[2, 0]
+    left2_ref[1] = swapped_ref[2, 1]
+
+
+def join(swapped, *own):
+    return pl.pallas_call(
+        join_kernel,
+        out_shape=[pltpu.VMEM((2 * a.shape[0],) + a.shape[1:], a.dtype) for a in own],
+        in_specs=[VMEM] * 5,
+        out_specs=[VMEM] * 4,
+        cost_estimate=pl.CostEstimate(flops=0, bytes_accessed=2 << 20, transcendentals=0),
+        compiler_params=pltpu.CompilerParams(vmem_limit_bytes=4 << 20),
+        name="join",
+    )(*in_vmem(swapped, *own))
 
 
 def turned(rows):
@@ -211,27 +255,21 @@
     pw, qw, w, albedo = maps
     sum_x, sum_y, sum_z, shade = totals
     sx, sy, sz, vx, vy, vz, mix, gain = values
-    mix2 = mix * 2.0
-    rest = 1.0 - mix
-    bright = bright.astype(jnp.float32)
+    mix2, rest = mix * 2.0, (1.0 - mix) * 0.5
+    vx, vy, vz = vx * 2.0, vy * 2.0, vz * 2.0
     ci = sz * w - sx * pw - sy * qw
     ce = vz * w - vx * pw - vy * qw
     square = ci * ci + SMOOTH
     inv_root = lax.rsqrt(square)
-    mu = (ci + square * inv_root) * 0.5
+    mu = ci + square * inv_root
     inv = 1.0 / (mu + ce)
     k = mix2 * inv
-    u = mu * inv
-    c = ce * inv
     shading = mu * (k + rest)
-    misfit = (gain * albedo) * shading - bright
-    scaled = gain * misfit
-    shade = shade + scaled * shading
-    gs = scaled * albedo
-    gk = gs * k
-    gl = gk * c + gs * rest
-    gi = gl * (mu * inv_root)
-    ge = gk * u
+    weight = gain * albedo
+    gs = weight * (weight * shading - bright.astype(jnp.float32))
+    shade = shade + gs * shading
+    gi = (gs * (k * (ce * inv) + rest)) * (mu * inv_root)
+    ge = (gs * k) * (mu * inv)
     return (
         sum_x + (gi * sx - ge * vx),
         sum_y + (gi * sy - ge * vy),
@@ -274,7 +312,7 @@
         up = (w * w * w) * (sum_z - p * sum_x - q * sum_y)
         half_x = (-(w * sum_x) - p * up) * (0.5 * scale)
         half_y = (-(w * sum_y) - q * up) * (0.5 * scale)
-        return half_x, half_y, shade * scale
+        return half_x, half_y, shade * scale / albedo
 
     def strip(index, carry):
         first = pl.multiple_of(index * STRIP, STRIP)
@@ -364,25 +402,19 @@
     tile_rows, tile_cols = heights.shape[1:]
     block_count = block_dest.shape[2]
 
-    params_wide = jnp.pad(
-        block_params.reshape(block_count, PARAMS).astype(jnp.float32), ((0, 0), (0, tile_cols - PARAMS))
-    )
     here = jnp.stack([lax.axis_index("zl"), lax.axis_index("c")]).astype(jnp.int32)
-    near, own, other = pack(
+    near, *own, other = pack(
         here,
         block_dest.reshape(block_count),
-        params_wide,
+        block_params.reshape(block_count, PARAMS).T,
         blocks.reshape(block_count, tile_rows, tile_cols),
     )
     swapped = lax.ppermute(other, "c", [(0, 1), (1, 0)])
-    to_right = jnp.concatenate([own[0], swapped[1]])
-    to_left = jnp.concatenate([own[2], swapped[3]])
-    to_right2 = jnp.stack([own[1, 0], swapped[2, 0]])
-    to_left2 = jnp.stack([own[1, 1], swapped[2, 1]])
+    to_right, to_left, to_right2, to_left2 = join(swapped, *own)
+    right2 = ring_shift(to_right2, 2)
+    left2 = ring_shift(to_left2, -2)
     right = ring_shift(to_right, 1)
     left = ring_shift(to_left, -1)
-    right2 = ring_shift(to_right2, 2)
-    left2 = ring_shift(to_left2, -2)
 
     height, shade = heights[0], albedo[0]
     first, last = jnp.stack([height[:, 0], height[:, 1], shade[:, 0]]), jnp.stack([height[:, -1], height[:, -2], shade[:, -1]])
@@ -397,8 +429,8 @@
     maps = make_maps(column, gathered)
 
     sums = terms(column, maps, None, [(near, [(0,), (1,)]), (swapped, [(0, 0), (0, 1)])], None)
-    sums = terms(column, maps, sums, [(right, EACH4), (left, EACH4)], None)
-    parts = terms(column, maps, sums, [(right2, EACH2), (left2, EACH2)], 1.0 / block_count)
+    sums = terms(column, maps, sums, [(right2, EACH2), (left2, EACH2)], None)
+    parts = terms(column, maps, sums, [(right, EACH4), (left, EACH4)], 1.0 / block_count)
     summed = jnp.sum(lax.all_to_all(parts, ("y",) + IMG, split_axis=0, concat_axis=0, tiled=True), axis=0)
     half = tile_rows // (HALVES * DEPTH)
     return (summed[None, :half], summed[None, half:])

time: 105 us -> 108 us (1.029)
  waiting for transfers between devices: 7.71 us -> 13.6 us
  local copies, waits for them, and re-layouts: 5.39 us -> 1.89 us
  other arithmetic: 3.49 us -> 0.32 us
  Pallas kernels: 18.1 us -> 20.4 us
  blocking collectives: 35 us -> 37.3 us
    ppermute x4, waiting for transfers between devices: 5.32 us -> 10.4 us  [ring_shift(): return lax.ppermute(value, ('zl', 'c', 'zh'), pairs)]
    unnamed x13 -> x4, local copies, waits for them, and re-layouts: 2.68 us -> 0.01 us
    all_to_all x1, blocking collectives: 35 us -> 37.3 us  [body(): lax.all_to_all(parts, ('y',) + IMG, split_axis=0, concat_axis=0, tiled=True)]
    concatenate x2 -> x0, other arithmetic: 1.7 us -> none  [the longest x1 0.85 us: body(): to_left = jnp.concatenate([own[2], swapped[3]])]
    another operation x2 -> x0, other arithmetic: 1.46 us -> none  [the longest x1 0.74 us: body(): to_left2 = jnp.stack([own[1, 1], swapped[2, 1]])]
    pallas_call x1, Pallas kernels: 4.18 us -> 5.64 us  [pack(): pl.pallas_call(pack_kernel, out_shape=[pltpu.VMEM(lead + unit, jnp.bfloat...]
    pallas_call x0 -> x1, Pallas kernels: none -> 1.3 us  [join(): pl.pallas_call(join_kernel, out_shape=[pltpu.VMEM((2 * a.shape[0],) + a.s...]
  transfers between devices with their start and end apart: 8 -> 8, of which waited for: 2 -> 3; matrix products, arithmetic and copies ran while one was open for 5% -> 1% of each run, Pallas kernels for 9% -> 8%
where the time goes in v2:
time: 108 us
  blocking collectives  37.3 us (35%)
  starting transfers between devices  33.4 us (31%)
  Pallas kernels  20.4 us (19%)
  waiting for transfers between devices  13.6 us (13%)
  local copies, waits for them, and re-layouts  1.89 us (2%)
    all_to_all x1, blocking collectives, body(): lax.all_to_all(parts, ('y',) + IMG, split_axis=0, concat_axis=0, tiled=True)  37.3 us
    ppermute x4, starting transfers between devices, ring_shift(): return lax.ppermute(value, ('zl', 'c', 'zh'), pairs)  20.7 us
    pallas_call x3, Pallas kernels, terms(): pl.pallas_call(lambda *refs: terms_kernel(scale, sums is not None, picks,...  13 us
    ppermute x4, waiting for transfers between devices, ring_shift(): return lax.ppermute(value, ('zl', 'c', 'zh'), pairs)  10.4 us
    all_to_all x1, starting transfers between devices, body(): lax.all_to_all(copies, 'y', split_axis=0, concat_axis=0, tiled=True)  7.1 us
    pallas_call x1, Pallas kernels, pack(): pl.pallas_call(pack_kernel, out_shape=[pltpu.VMEM(lead + unit, jnp.bfloat...  5.64 us
    ppermute x2, starting transfers between devices, column_shift(): return lax.ppermute(value, ('zl', 'c'), pairs)  3.69 us
    ppermute x2, waiting for transfers between devices, column_shift(): return lax.ppermute(value, ('zl', 'c'), pairs)  3.18 us
  transfers between devices with their start and end apart: 8, of which 3 were waited for; matrix products, arithmetic and copies ran while one was open for 1% of the time, Pallas kernels for 8%

profile of v2, /device:TPU:6, one launch (start us, length us, event | category | flops | bytes accessed | tf_op | source)
XLA Modules:
  0.0 107.8 jit_solution(7598046121850945953)
XLA Ops:
  0.6 0.0 copy-start.1
  0.7 0.1 pad_add_fusion.here_ref
  0.7 5.6 %pack.1 = (bf16[2,528,128]{2,1,0:T(8,128)(2,1)S(1)}, bf16[2,528,128]{2,1,0:T(8,128)(2,1)S(1)}, bf16[2,528,128]{2,1,0:T(8,128)(2,1)S(1)}, bf16[1,528,128]{2,1,0:T...) custom-call(s32[2]{0:T(128)S(1)} %pad_add_fusion.here_ref, s32[64]{0:T(128)} %bitcast.34, ...), custom_call_target="tpu_custom_call" | custom-call | bytes 6291456 | tf_op jit(solution)/shard_map/pack/pallas_call | solution.py:143
  6.4 1.9 %collective-permute-start.2 = (bf16[4,2,528,128]{3,2,1,0:T(8,128)(2,1)}, bf16[4,2,528,128]{3,2,1,0:T(8,128)(2,1)S(1)}, u32[]{:S(2)}, u32[]{:S(2)}) collective-permute-start(bf16[4,2,528,128]{3,2,1,0:T(8,128)(2,1)} %get-tuple-element.13), channel_id=1, source_target_pairs={{0,8},{8,0},{1,9},{9,1},{2,10},{10,2},{3,11},{11,3},{4,12},{12,4},... | collective-permute-start | bytes 3244040 | tf_op jit(solution)/shard_map/ppermute | solution.py:412
  8.3 0.2 slice_reduce_fusion.3
  8.5 0.2 slice_reduce_fusion.5
  8.7 2.4 %collective-permute-start = (f32[3,64]{1,0:T(4,128)S(1)}, f32[3,64]{1,0:T(4,128)S(1)}, u32[]{:S(2)}, u32[]{:S(2)}) collective-permute-start(f32[3,64]{1,0:T(4,128)S(1)} %pad_maximum_fusion), channel_id=1, source_target_pairs={{0,8},{8,16},{16,24},{24,32},{32,40},{40,48},{48,56},{1,9},{9,17},... | collective-permute-start | bytes 2312 | tf_op jit(solution)/shard_map/ppermute | solution.py:36
  11.2 1.3 %collective-permute-start.1 = (f32[3,64]{1,0:T(4,128)S(1)}, f32[3,64]{1,0:T(4,128)S(1)}, u32[]{:S(2)}, u32[]{:S(2)}) collective-permute-start(f32[3,64]{1,0:T(4,128)S(1)} %pad_maximum_fusion.1), channel_id=1, source_target_pairs={{8,0},{16,8},{24,16},{32,24},{40,32},{48,40},{56,48},{9,1},{17,9},... | collective-permute-start | bytes 2312 | tf_op jit(solution)/shard_map/ppermute | solution.py:36
  12.5 0.1 pad_maximum_fusion.3
  12.5 0.0 collective-permute-done
  12.5 3.2 %collective-permute-done.1 = f32[3,64]{1,0:T(4,128)S(1)} collective-permute-done((f32[3,64]{1,0:T(4,128)S(1)}, f32[3,64]{1,0:T(4,128)S(1)}, u32[]{:S(2)}, u32[]{:S(2)}) %collective-permute-start.1) | collective-permute-done | bytes 800 | tf_op jit(solution)/shard_map/ppermute | solution.py:36
  15.7 0.1 pad_maximum_fusion.2
  15.8 0.9 broadcast_in_dim.16
  16.7 7.1 %all-to-all-start = ((f32[8,136,128]{2,1,0:T(8,128)}), f32[8,136,128]{2,1,0:T(8,128)S(1)}, u32[]{:S(2)}, u32[]{:S(2)}) async-start(f32[8,136,128]{2,1,0:T(8,128)} %broadcast_in_dim.16), calls=%async_computation | async-start | bytes 1114112 | tf_op jit(solution)/shard_map/all_to_all | solution.py:427
  23.8 0.0 collective-permute-done.2.refs_3_.swapped_ref
  23.8 1.3 %join.1 = (bf16[4,528,128]{2,1,0:T(8,128)(2,1)}, bf16[4,528,128]{2,1,0:T(8,128)(2,1)}, bf16[2,528,128]{2,1,0:T(8,128)(2,1)}, bf16[2,528,128]{2,1,0:T(8,128)(2,1)}) custom-call(bf16[4,2,528,128]{3,2,1,0:T(8,128)(2,1)S(1)} %collective-permute-done.2.refs_3_.swapped_ref, bf16[2,528,128]{2,1,0:T(8,128)(2,1)S(1)} %get-tuple-element.14.refs_0_, ...), custom_call_target="tpu_custom_call" | custom-call | bytes 2097152 | tf_op jit(solution)/shard_map/join/pallas_call | solution.py:174
  25.1 4.3 %collective-permute-start.5 = (bf16[4,528,128]{2,1,0:T(8,128)(2,1)}, bf16[4,528,128]{2,1,0:T(8,128)(2,1)S(1)}, u32[]{:S(2)}, u32[]{:S(2)}) collective-permute-start(bf16[4,528,128]{2,1,0:T(8,128)(2,1)} %get-tuple-element.20), channel_id=1, source_target_pairs={{0,16},{4,20},{8,24},{12,28},{16,32},{20,36},{24,40},{28,44},{32,4... | collective-permute-start | bytes 1622024 | tf_op jit(solution)/shard_map/ppermute | solution.py:30
  29.4 8.5 %collective-permute-start.6 = (bf16[4,528,128]{2,1,0:T(8,128)(2,1)}, bf16[4,528,128]{2,1,0:T(8,128)(2,1)S(1)}, u32[]{:S(2)}, u32[]{:S(2)}) collective-permute-start(bf16[4,528,128]{2,1,0:T(8,128)(2,1)} %get-tuple-element.21), channel_id=1, source_target_pairs={{0,52},{4,48},{8,60},{12,56},{16,0},{20,4},{24,8},{28,12},{32,16},... | collective-permute-start | bytes 1622024 | tf_op jit(solution)/shard_map/ppermute | solution.py:30
  37.9 1.9 %collective-permute-start.3 = (bf16[2,528,128]{2,1,0:T(8,128)(2,1)}, bf16[2,528,128]{2,1,0:T(8,128)(2,1)S(1)}, u32[]{:S(2)}, u32[]{:S(2)}) collective-permute-start(bf16[2,528,128]{2,1,0:T(8,128)(2,1)} %get-tuple-element.18), channel_id=1, source_target_pairs={{0,32},{4,36},{8,40},{12,44},{16,48},{20,52},{24,56},{28,60},{32,4... | collective-permute-start | bytes 811016 | tf_op jit(solution)/shard_map/ppermute | solution.py:30
  39.8 6.0 %collective-permute-start.4 = (bf16[2,528,128]{2,1,0:T(8,128)(2,1)}, bf16[2,528,128]{2,1,0:T(8,128)(2,1)S(1)}, u32[]{:S(2)}, u32[]{:S(2)}) collective-permute-start(bf16[2,528,128]{2,1,0:T(8,128)(2,1)} %get-tuple-element.19), channel_id=1, source_target_pairs={{0,36},{4,32},{8,44},{12,40},{16,52},{20,48},{24,60},{28,56},{32,0... | collective-permute-start | bytes 811016 | tf_op jit(solution)/shard_map/ppermute | solution.py:30
  45.8 0.0 all-to-all-done.got_ref
  45.8 0.4 maps.1.refs_1_
  46.3 3.3 %shard_map.68.refs_2_ = f32[4,520,128]{2,1,0:T(8,128)S(1)} custom-call(s32[1]{0:T(128)} %bitcast.column_ref.refs_0_, f32[4,520,128]{2,1,0:T(8,128)S(1)} %maps.1.refs_1_, bf16[2,528,128]{2,1,0:T(8,128)(2,1)S(1)} %get-tuple-element.12.refs_2_, bf16[4,2,528,128]{3,2,1,0:T(8,128)(2,1)S(1)} %collective-permute-done.2.refs_3_.swapped_ref), custom_call_target="tpu_custom_call" | custom-call | flops 15974400 | bytes 4194304 | tf_op jit(solution)/shard_map/pallas_call | solution.py:385
  49.6 6.6 %collective-permute-done.3.refs_3_ = bf16[2,528,128]{2,1,0:T(8,128)(2,1)S(1)} collective-permute-done((bf16[2,528,128]{2,1,0:T(8,128)(2,1)}, bf16[2,528,128]{2,1,0:T(8,128)(2,1)S(1)}, u32[]{:S(2)}, u32[]{:S(2)}) %collective-permute-start.3) | collective-permute-done | bytes 270368 | tf_op jit(solution)/shard_map/ppermute | solution.py:30
  56.1 3.8 %collective-permute-done.4.refs_4_ = bf16[2,528,128]{2,1,0:T(8,128)(2,1)S(1)} collective-permute-done((bf16[2,528,128]{2,1,0:T(8,128)(2,1)}, bf16[2,528,128]{2,1,0:T(8,128)(2,1)S(1)}, u32[]{:S(2)}, u32[]{:S(2)}) %collective-permute-start.4) | collective-permute-done | bytes 270368 | tf_op jit(solution)/shard_map/ppermute | solution.py:30
  60.0 3.3 %shard_map.69.refs_2_ = f32[4,520,128]{2,1,0:T(8,128)S(1)} custom-call(s32[1]{0:T(128)} %bitcast.column_ref.refs_0_, f32[4,520,128]{2,1,0:T(8,128)S(1)} %maps.1.refs_1_, f32[4,520,128]{2,1,0:T(8,128)S(1)} %shard_map.68.refs_2_, bf16[2,528,128]{2,1,0:T(8,128)(2,1)S(1)} %collective-permute-done.3.refs_3_, bf16[2,528,128]{2,1,0:T(8,128)(2,1)S(1)} %collective-permute-done.4.refs_4_), custom_call_target="tpu_custom_call" | custom-call | flops 15974400 | bytes 4194304 | tf_op jit(solution)/shard_map/pallas_call | solution.py:385
  63.3 0.0 collective-permute-done.5.refs_3_
  63.3 0.0 collective-permute-done.6.refs_4_
  63.3 6.5 %shard_map.70 = f32[64,16,128]{2,1,0:T(8,128)S(1)} custom-call(s32[1]{0:T(128)} %bitcast.column_ref.refs_0_, f32[4,520,128]{2,1,0:T(8,128)S(1)} %maps.1.refs_1_, f32[4,520,128]{2,1,0:T(8,128)S(1)} %shard_map.69.refs_2_, bf16[4,528,128]{2,1,0:T(8,128)(2,1)S(1)} %collective-permute-done.5.refs_3_, bf16[4,528,128]{2,1,0:T(8,128)(2,1)S(1)} %collective-permute-done.6.refs_4_), custom_call_target="tpu_custom_call" | custom-call | flops 31948800 | bytes 4194304 | tf_op jit(solution)/shard_map/pallas_call | solution.py:385
  69.8 37.3 %all_to_all.10 = f32[64,16,128]{2,1,0:T(8,128)S(1)} all-to-all(f32[64,16,128]{2,1,0:T(8,128)S(1)} %shard_map.70), channel_id=1, replica_groups=mesh['y'=8,'zl'=4,'c'=2,'zh'=2,'x'=4] {'y','zh','x'}, dimensions={0} | all-to-all | bytes 1048576 | tf_op jit(solution)/shard_map/all_to_all | solution.py:434
  107.1 0.1 reduce_sum.9
  107.2 0.6 slice_bitcast_fusion
  (7 shorter events, 0.1 us)
Async XLA Ops:
  0.6 7.7 %copy-start.1 = (f32[1,64,128]{2,1,0:T(8,128)S(1)}, f32[1,64,128]{2,1,0:T(8,128)}, u32[]{:S(2)}) copy-start(f32[1,64,128]{2,1,0:T(8,128)} %param.6) | copy-start | bytes 98308
  0.6 7.9 %copy-start = (f32[1,64,128]{2,1,0:T(8,128)S(1)}, f32[1,64,128]{2,1,0:T(8,128)}, u32[]{:S(2)}) copy-start(f32[1,64,128]{2,1,0:T(8,128)} %param.5) | copy-start | bytes 98308
  6.4 17.4 %collective-permute-start.2 = (bf16[4,2,528,128]{3,2,1,0:T(8,128)(2,1)}, bf16[4,2,528,128]{3,2,1,0:T(8,128)(2,1)S(1)}, u32[]{:S(2)}, u32[]{:S(2)}) collective-permute-start(bf16[4,2,528,128]{3,2,1,0:T(8,128)(2,1)} %get-tuple-element.13), channel_id=1, source_target_pairs={{0,8},{8,0},{1,9},{9,1},{2,10},{10,2},{3,11},{11,3},{4,12},{12,4},... | collective-permute-start | bytes 3244040 | tf_op jit(solution)/shard_map/ppermute | solution.py:412
  8.7 3.8 %collective-permute-start = (f32[3,64]{1,0:T(4,128)S(1)}, f32[3,64]{1,0:T(4,128)S(1)}, u32[]{:S(2)}, u32[]{:S(2)}) collective-permute-start(f32[3,64]{1,0:T(4,128)S(1)} %pad_maximum_fusion), channel_id=1, source_target_pairs={{0,8},{8,16},{16,24},{24,32},{32,40},{40,48},{48,56},{1,9},{9,17},... | collective-permute-start | bytes 2312 | tf_op jit(solution)/shard_map/ppermute | solution.py:36
  11.2 4.6 %collective-permute-start.1 = (f32[3,64]{1,0:T(4,128)S(1)}, f32[3,64]{1,0:T(4,128)S(1)}, u32[]{:S(2)}, u32[]{:S(2)}) collective-permute-start(f32[3,64]{1,0:T(4,128)S(1)} %pad_maximum_fusion.1), channel_id=1, source_target_pairs={{8,0},{16,8},{24,16},{32,24},{40,32},{48,40},{56,48},{9,1},{17,9},... | collective-permute-start | bytes 2312 | tf_op jit(solution)/shard_map/ppermute | solution.py:36
  16.7 29.2 %all-to-all-start = ((f32[8,136,128]{2,1,0:T(8,128)}), f32[8,136,128]{2,1,0:T(8,128)S(1)}, u32[]{:S(2)}, u32[]{:S(2)}) async-start(f32[8,136,128]{2,1,0:T(8,128)} %broadcast_in_dim.16), calls=%async_computation | async-start | bytes 1114112 | tf_op jit(solution)/shard_map/all_to_all | solution.py:427
  25.1 38.2 %collective-permute-start.5 = (bf16[4,528,128]{2,1,0:T(8,128)(2,1)}, bf16[4,528,128]{2,1,0:T(8,128)(2,1)S(1)}, u32[]{:S(2)}, u32[]{:S(2)}) collective-permute-start(bf16[4,528,128]{2,1,0:T(8,128)(2,1)} %get-tuple-element.20), channel_id=1, source_target_pairs={{0,16},{4,20},{8,24},{12,28},{16,32},{20,36},{24,40},{28,44},{32,4... | collective-permute-start | bytes 1622024 | tf_op jit(solution)/shard_map/ppermute | solution.py:30
  29.4 33.9 %collective-permute-start.6 = (bf16[4,528,128]{2,1,0:T(8,128)(2,1)}, bf16[4,528,128]{2,1,0:T(8,128)(2,1)S(1)}, u32[]{:S(2)}, u32[]{:S(2)}) collective-permute-start(bf16[4,528,128]{2,1,0:T(8,128)(2,1)} %get-tuple-element.21), channel_id=1, source_target_pairs={{0,52},{4,48},{8,60},{12,56},{16,0},{20,4},{24,8},{28,12},{32,16},... | collective-permute-start | bytes 1622024 | tf_op jit(solution)/shard_map/ppermute | solution.py:30
  37.9 18.3 %collective-permute-start.3 = (bf16[2,528,128]{2,1,0:T(8,128)(2,1)}, bf16[2,528,128]{2,1,0:T(8,128)(2,1)S(1)}, u32[]{:S(2)}, u32[]{:S(2)}) collective-permute-start(bf16[2,528,128]{2,1,0:T(8,128)(2,1)} %get-tuple-element.18), channel_id=1, source_target_pairs={{0,32},{4,36},{8,40},{12,44},{16,48},{20,52},{24,56},{28,60},{32,4... | collective-permute-start | bytes 811016 | tf_op jit(solution)/shard_map/ppermute | solution.py:30
  39.8 20.2 %collective-permute-start.4 = (bf16[2,528,128]{2,1,0:T(8,128)(2,1)}, bf16[2,528,128]{2,1,0:T(8,128)(2,1)S(1)}, u32[]{:S(2)}, u32[]{:S(2)}) collective-permute-start(bf16[2,528,128]{2,1,0:T(8,128)(2,1)} %get-tuple-element.19), channel_id=1, source_target_pairs={{0,36},{4,32},{8,44},{12,40},{16,52},{20,48},{24,60},{28,56},{32,0... | collective-permute-start | bytes 811016 | tf_op jit(solution)/shard_map/ppermute | solution.py:30

commit v3 on v2

--- a/solution.py
+++ b/solution.py
@@ -57,7 +57,7 @@
 
 
 def pack_kernel(
-    here_ref, dest_ref, params_ref, blocks_hbm, near_ref, right_ref, left_ref, right2_ref, left2_ref, other_ref,
+    here_ref, dest_ref, params_ref, height_ref, albedo_ref, blocks_hbm, near_ref, right_ref, left_ref, right2_ref, left2_ref, other_ref, copies_ref,
     blocks_ref, sem, table, shifted, columns, rim, lines,
 ):
     number, tile_rows, tile_cols = blocks_ref.shape
@@ -69,6 +69,20 @@
     plain = turned(upright)[:number]
     for k in range(3):
         shifted[k] = plain if k == 0 else pltpu.roll(plain, k * PARAMS, 1)
+
+    height, albedo = height_ref[...], albedo_ref[...]
+    blank = jnp.zeros((tile_cols - tile_rows, tile_cols), jnp.float32)
+    tall, shade = (jnp.transpose(jnp.concatenate([m, blank])) for m in (height, albedo))
+    west_half = lax.broadcasted_iota(jnp.int32, (1, tile_cols), 1) < tile_rows
+    ends = [
+        jnp.where(west_half, m[a : a + 1], pltpu.roll(m[b : b + 1], tile_rows, 1))
+        for m, a, b in ((tall, 0, tile_cols - 1), (tall, 1, tile_cols - 2), (shade, 0, tile_cols - 1))
+    ]
+    ends = jnp.concatenate(ends + [jnp.zeros((ROWS - 3, tile_cols), jnp.float32)])
+    for row in range(ROWS):
+        copies_ref[row, :tile_rows, :] = height
+        copies_ref[row, tile_rows : 2 * tile_rows, :] = albedo
+        copies_ref[row, 2 * tile_rows :, :] = ends
     fetch.wait()
 
     lane8 = lax.broadcasted_iota(jnp.int32, (8, tile_cols), 1)
@@ -92,7 +106,6 @@
 
     low, core = here_ref[0], here_ref[1]
     count = CLASSES * CORES
-    west_half = lax.broadcasted_iota(jnp.int32, (1, tile_cols), 1) < tile_rows
     pixels = ROWS * tile_rows
     mine = {
         0: (near_ref.at[0], near_ref.at[1]),
@@ -137,14 +150,15 @@
                     units[slot][pixels + k * ROWS : pixels + (k + 1) * ROWS, :] = lines[k, slot].astype(jnp.bfloat16)
 
 
-def pack(here, dest, params, blocks):
+def pack(here, dest, params, height, albedo, blocks):
     number, tile_rows, tile_cols = blocks.shape
     unit = (ROWS * tile_rows + 2 * ROWS, tile_cols)
     return pl.pallas_call(
         pack_kernel,
-        out_shape=[pltpu.VMEM(lead + unit, jnp.bfloat16) for lead in ((2,), (2,), (2,), (1,), (1,), (CLASSES, 2))],
-        in_specs=[SMEM, SMEM, VMEM, pl.BlockSpec(memory_space=pltpu.HBM)],
-        out_specs=[VMEM] * 6,
+        out_shape=[pltpu.VMEM(lead + unit, jnp.bfloat16) for lead in ((2,), (2,), (2,), (1,), (1,), (CLASSES, 2))]
+        + [pltpu.VMEM((ROWS, 2 * tile_rows + ROWS, tile_cols), jnp.float32)],
+        in_specs=[SMEM, SMEM, VMEM, VMEM, VMEM, pl.BlockSpec(memory_space=pltpu.HBM)],
+        out_specs=[VMEM] * 7,
         scratch_shapes=[
             pltpu.VMEM(blocks.shape, jnp.bfloat16),
             pltpu.SemaphoreType.DMA,
@@ -157,7 +171,7 @@
         cost_estimate=pl.CostEstimate(flops=0, bytes_accessed=6 << 20, transcendentals=0),
         compiler_params=pltpu.CompilerParams(vmem_limit_bytes=8 << 20),
         name="pack",
-    )(here, *[pltpu.with_memory_space_constraint(a, pltpu.HBM) for a in (dest, params, blocks)])
+    )(here, *[pltpu.with_memory_space_constraint(a, pltpu.HBM) for a in (dest, params, height, albedo, blocks)])
 
 
 def join_kernel(swapped_ref, *refs):
@@ -187,7 +201,7 @@
     return jnp.transpose(jnp.concatenate([rows, jnp.zeros((size - rows.shape[0], size), rows.dtype)]))
 
 
-def maps_kernel(column_ref, got_ref, maps_ref, tall, side):
+def maps_kernel(column_ref, got_ref, west_ref, east_ref, maps_ref, tall, side):
     tile_cols = got_ref.shape[2]
     tile_rows = (got_ref.shape[1] - ROWS) // 2
     pixels = ROWS * tile_rows
@@ -204,9 +218,11 @@
         tall[8 + row * tile_rows : 8 + (row + 1) * tile_rows, :] = got_ref[row, :tile_rows, :]
     tall[7:8, :] = got_ref[0, 0:1, :]
     tall[8 + pixels : 9 + pixels, :] = got_ref[ROWS - 1, tile_rows - 1 : tile_rows, :]
-    beside, beyond, shade, mine = [
-        jnp.concatenate([got_ref[row, 2 * tile_rows + k : 2 * tile_rows + k + 1, :] for row in range(ROWS)]) for k in range(4)
+    left_half = lax.broadcasted_iota(jnp.int32, (ROWS, tile_cols), 1) < tile_rows
+    beside, beyond, shade = [
+        pltpu.roll(jnp.where(left_half, east_ref[k], west_ref[k]), tile_rows, 1) for k in range(3)
     ]
+    mine = jnp.concatenate([got_ref[row, 2 * tile_rows : 2 * tile_rows + 1, :] for row in range(ROWS)])
     side[...] = turned(beside)
     for row in range(ROWS):
         start = 8 + row * tile_rows
@@ -233,13 +249,13 @@
     finish(slice(pixels, pixels + ROWS), p, (following - preceding) * 0.5, shade)
 
 
-def make_maps(column, got):
+def make_maps(column, got, from_west, from_east):
     tile_cols = got.shape[2]
     pixels = ROWS * (got.shape[1] - ROWS) // 2
     return pl.pallas_call(
         maps_kernel,
         out_shape=pltpu.VMEM((4, pixels + ROWS, tile_cols), jnp.float32),
-        in_specs=[SMEM, VMEM],
+        in_specs=[SMEM, VMEM, VMEM, VMEM],
         out_specs=VMEM,
         scratch_shapes=[
             pltpu.VMEM((pixels + 16, tile_cols), jnp.float32),
@@ -248,7 +264,7 @@
         cost_estimate=pl.CostEstimate(flops=0, bytes_accessed=3 << 20, transcendentals=0),
         compiler_params=pltpu.CompilerParams(vmem_limit_bytes=4 << 20),
         name="maps",
-    )(column, *in_vmem(got))
+    )(column, *in_vmem(got, from_west, from_east))
 
 
 def add_block(maps, totals, values, bright):
@@ -403,10 +419,12 @@
     block_count = block_dest.shape[2]
 
     here = jnp.stack([lax.axis_index("zl"), lax.axis_index("c")]).astype(jnp.int32)
-    near, *own, other = pack(
+    near, *own, other, copies = pack(
         here,
         block_dest.reshape(block_count),
         block_params.reshape(block_count, PARAMS).T,
+        heights[0],
+        albedo[0],
         blocks.reshape(block_count, tile_rows, tile_cols),
     )
     swapped = lax.ppermute(other, "c", [(0, 1), (1, 0)])
@@ -416,21 +434,17 @@
     right = ring_shift(to_right, 1)
     left = ring_shift(to_left, -1)
 
-    height, shade = heights[0], albedo[0]
-    first, last = jnp.stack([height[:, 0], height[:, 1], shade[:, 0]]), jnp.stack([height[:, -1], height[:, -2], shade[:, -1]])
-    from_west = column_shift(last, 1)
-    from_east = column_shift(first, -1)
-    beside = jnp.concatenate([from_west, from_east], axis=1)
-    mine = jnp.concatenate([first[:1], last[:1]], axis=1)
-    rows = jnp.concatenate([beside, mine, jnp.zeros((ROWS - 4, tile_cols), jnp.float32)])
-    copies = jnp.broadcast_to(jnp.concatenate([height, shade, rows])[None], (ROWS, 2 * tile_rows + ROWS, tile_cols))
     gathered = lax.all_to_all(copies, "y", split_axis=0, concat_axis=0, tiled=True)
+    ends = gathered[:, 2 * tile_rows : 2 * tile_rows + 3].swapaxes(0, 1)
+    from_west = column_shift(ends, 1)
+    from_east = column_shift(ends, -1)
     column = column_here.reshape(1).astype(jnp.int32)
-    maps = make_maps(column, gathered)
+    maps = make_maps(column, gathered, from_west, from_east)
 
     sums = terms(column, maps, None, [(near, [(0,), (1,)]), (swapped, [(0, 0), (0, 1)])], None)
     sums = terms(column, maps, sums, [(right2, EACH2), (left2, EACH2)], None)
-    parts = terms(column, maps, sums, [(right, EACH4), (left, EACH4)], 1.0 / block_count)
+    sums = terms(column, maps, sums, [(right, EACH4)], None)
+    parts = terms(column, maps, sums, [(left, EACH4)], 1.0 / block_count)
     summed = jnp.sum(lax.all_to_all(parts, ("y",) + IMG, split_axis=0, concat_axis=0, tiled=True), axis=0)
     half = tile_rows // (HALVES * DEPTH)
     return (summed[None, :half], summed[None, half:])

time: 108 us -> 106 us (0.981)
  the two profiles are of different devices: /device:TPU:6 before, /device:TPU:70 now
where the time goes in v3:
time: 106 us; the launch traced here: 105 us
  blocking collectives  37.4 us (35%)
  starting transfers between devices  37.2 us (35%)
  Pallas kernels  21.6 us (20%)
  waiting for transfers between devices  7.12 us (7%)
  local copies, waits for them, and re-layouts  1.2 us (1%)
    all_to_all x1, blocking collectives, body(): lax.all_to_all(parts, ('y',) + IMG, split_axis=0, concat_axis=0, tiled=True)  37.4 us
    ppermute x4, starting transfers between devices, ring_shift(): return lax.ppermute(value, ('zl', 'c', 'zh'), pairs)  17.8 us
    pallas_call x4, Pallas kernels, terms(): pl.pallas_call(lambda *refs: terms_kernel(scale, sums is not None, picks,...  14 us
    ppermute x2, starting transfers between devices, column_shift(): return lax.ppermute(value, ('zl', 'c'), pairs)  10.4 us
    all_to_all x1, starting transfers between devices, body(): lax.all_to_all(copies, 'y', split_axis=0, concat_axis=0, tiled=True)  7.11 us
    ppermute x2, waiting for transfers between devices, column_shift(): return lax.ppermute(value, ('zl', 'c'), pairs)  7.1 us
    pallas_call x1, Pallas kernels, pack(): pl.pallas_call(pack_kernel, out_shape=[pltpu.VMEM(lead + unit, jnp.bfloat...  5.94 us
  transfers between devices with their start and end apart: 8, of which 2 were waited for; matrix products, arithmetic and copies ran while one was open for 1% of the time, Pallas kernels for 11%

profile of v3, /device:TPU:70, one launch (start us, length us, event | category | flops | bytes accessed | tf_op | source)
XLA Modules:
  0.0 105.5 jit_solution(13754384611501151137)
XLA Ops:
  0.6 0.1 pad_add_fusion.here_ref
  0.7 5.9 %pack.1 = (bf16[2,528,128]{2,1,0:T(8,128)(2,1)S(1)}, bf16[2,528,128]{2,1,0:T(8,128)(2,1)S(1)}, bf16[2,528,128]{2,1,0:T(8,128)(2,1)S(1)}, bf16[1,528,128]{2,1,0:T...) custom-call(s32[2]{0:T(128)S(1)} %pad_add_fusion.here_ref, ...), custom_call_target="tpu_custom_call" | custom-call | bytes 6291456 | tf_op jit(solution)/shard_map/pack/pallas_call | solution.py:156
  6.7 1.9 %collective-permute-start.2 = (bf16[4,2,528,128]{3,2,1,0:T(8,128)(2,1)}, bf16[4,2,528,128]{3,2,1,0:T(8,128)(2,1)S(1)}, u32[]{:S(2)}, u32[]{:S(2)}) collective-permute-start(bf16[4,2,528,128]{3,2,1,0:T(8,128)(2,1)} %get-tuple-element.15), channel_id=1, source_target_pairs={{0,8},{8,0},{1,9},{9,1},{2,10},{10,2},{3,11},{11,3},{4,12},{12,4},... | collective-permute-start | bytes 3244040 | tf_op jit(solution)/shard_map/ppermute | solution.py:430
  8.6 7.1 %all-to-all-start = ((f32[8,136,128]{2,1,0:T(8,128)}), f32[8,136,128]{2,1,0:T(8,128)S(1)}, u32[]{:S(2)}, u32[]{:S(2)}) async-start(f32[8,136,128]{2,1,0:T(8,128)} %get-tuple-element.13), calls=%async_computation | async-start | bytes 1114112 | tf_op jit(solution)/shard_map/all_to_all | solution.py:437
  15.7 0.0 collective-permute-done.2.refs_3_.swapped_ref
  15.7 1.3 %join.1 = (bf16[4,528,128]{2,1,0:T(8,128)(2,1)}, bf16[4,528,128]{2,1,0:T(8,128)(2,1)}, bf16[2,528,128]{2,1,0:T(8,128)(2,1)}, bf16[2,528,128]{2,1,0:T(8,128)(2,1)}) custom-call(bf16[4,2,528,128]{3,2,1,0:T(8,128)(2,1)S(1)} %collective-permute-done.2.refs_3_.swapped_ref, bf16[2,528,128]{2,1,0:T(8,128)(2,1)S(1)} %get-tuple-element.16.refs_0_, ...), custom_call_target="tpu_custom_call" | custom-call | bytes 2097152 | tf_op jit(solution)/shard_map/join/pallas_call | solution.py:188
  17.0 4.3 %collective-permute-start.5 = (bf16[4,528,128]{2,1,0:T(8,128)(2,1)}, bf16[4,528,128]{2,1,0:T(8,128)(2,1)S(1)}, u32[]{:S(2)}, u32[]{:S(2)}) collective-permute-start(bf16[4,528,128]{2,1,0:T(8,128)(2,1)} %get-tuple-element.22), channel_id=1, source_target_pairs={{0,16},{4,20},{8,24},{12,28},{16,32},{20,36},{24,40},{28,44},{32,4... | collective-permute-start | bytes 1622024 | tf_op jit(solution)/shard_map/ppermute | solution.py:30
  21.2 1.9 %collective-permute-start.6 = (bf16[4,528,128]{2,1,0:T(8,128)(2,1)}, bf16[4,528,128]{2,1,0:T(8,128)(2,1)S(1)}, u32[]{:S(2)}, u32[]{:S(2)}) collective-permute-start(bf16[4,528,128]{2,1,0:T(8,128)(2,1)} %get-tuple-element.23), channel_id=1, source_target_pairs={{0,52},{4,48},{8,60},{12,56},{16,0},{20,4},{24,8},{28,12},{32,16},... | collective-permute-start | bytes 1622024 | tf_op jit(solution)/shard_map/ppermute | solution.py:30
  23.2 7.3 %collective-permute-start.3 = (bf16[2,528,128]{2,1,0:T(8,128)(2,1)}, bf16[2,528,128]{2,1,0:T(8,128)(2,1)S(1)}, u32[]{:S(2)}, u32[]{:S(2)}) collective-permute-start(bf16[2,528,128]{2,1,0:T(8,128)(2,1)} %get-tuple-element.20), channel_id=1, source_target_pairs={{0,32},{4,36},{8,40},{12,44},{16,48},{20,52},{24,56},{28,60},{32,4... | collective-permute-start | bytes 811016 | tf_op jit(solution)/shard_map/ppermute | solution.py:30
  30.5 4.3 %collective-permute-start.4 = (bf16[2,528,128]{2,1,0:T(8,128)(2,1)}, bf16[2,528,128]{2,1,0:T(8,128)(2,1)S(1)}, u32[]{:S(2)}, u32[]{:S(2)}) collective-permute-start(bf16[2,528,128]{2,1,0:T(8,128)(2,1)} %get-tuple-element.21), channel_id=1, source_target_pairs={{0,36},{4,32},{8,44},{12,40},{16,52},{20,48},{24,60},{28,56},{32,0... | collective-permute-start | bytes 811016 | tf_op jit(solution)/shard_map/ppermute | solution.py:30
  34.8 0.0 all-to-all-done.got_ref
  34.8 0.6 copy.12
  35.4 3.6 %collective-permute-start.1 = (f32[3,8,128]{2,1,0:T(8,128)}, f32[3,8,128]{2,1,0:T(8,128)S(1)}, u32[]{:S(2)}, u32[]{:S(2)}) collective-permute-start(f32[3,8,128]{2,1,0:T(8,128)} %bitcast.16), channel_id=1, source_target_pairs={{8,0},{16,8},{24,16},{32,24},{40,32},{48,40},{56,48},{9,1},{17,9},... | collective-permute-start | bytes 36872 | tf_op jit(solution)/shard_map/ppermute | solution.py:36
  39.0 6.1 %collective-permute-done.1.east_ref = f32[3,8,128]{2,1,0:T(8,128)S(1)} collective-permute-done((f32[3,8,128]{2,1,0:T(8,128)}, f32[3,8,128]{2,1,0:T(8,128)S(1)}, u32[]{:S(2)}, u32[]{:S(2)}) %collective-permute-start.1) | collective-permute-done | bytes 12320 | tf_op jit(solution)/shard_map/ppermute | solution.py:36
  45.0 6.8 %collective-permute-start = (f32[3,8,128]{2,1,0:T(8,128)}, f32[3,8,128]{2,1,0:T(8,128)S(1)}, u32[]{:S(2)}, u32[]{:S(2)}) collective-permute-start(f32[3,8,128]{2,1,0:T(8,128)} %bitcast.16), channel_id=1, source_target_pairs={{0,8},{8,16},{16,24},{24,32},{32,40},{40,48},{48,56},{1,9},{9,17},... | collective-permute-start | bytes 36872 | tf_op jit(solution)/shard_map/ppermute | solution.py:36
  51.9 1.0 collective-permute-done.west_ref
  52.9 0.5 maps.1.refs_1_
  53.4 3.3 %shard_map.68.refs_2_ = f32[4,520,128]{2,1,0:T(8,128)S(1)} custom-call(s32[1]{0:T(128)} %bitcast.column_ref.refs_0_, f32[4,520,128]{2,1,0:T(8,128)S(1)} %maps.1.refs_1_, bf16[2,528,128]{2,1,0:T(8,128)(2,1)S(1)} %get-tuple-element.14.refs_2_, bf16[4,2,528,128]{3,2,1,0:T(8,128)(2,1)S(1)} %collective-permute-done.2.refs_3_.swapped_ref), custom_call_target="tpu_custom_call" | custom-call | flops 15974400 | bytes 4194304 | tf_op jit(solution)/shard_map/pallas_call | solution.py:401
  56.6 0.0 collective-permute-done.3.refs_3_
  56.6 0.0 collective-permute-done.4.refs_4_
  56.7 3.3 %shard_map.69.refs_2_ = f32[4,520,128]{2,1,0:T(8,128)S(1)} custom-call(s32[1]{0:T(128)} %bitcast.column_ref.refs_0_, f32[4,520,128]{2,1,0:T(8,128)S(1)} %maps.1.refs_1_, f32[4,520,128]{2,1,0:T(8,128)S(1)} %shard_map.68.refs_2_, bf16[2,528,128]{2,1,0:T(8,128)(2,1)S(1)} %collective-permute-done.3.refs_3_, bf16[2,528,128]{2,1,0:T(8,128)(2,1)S(1)} %collective-permute-done.4.refs_4_), custom_call_target="tpu_custom_call" | custom-call | flops 15974400 | bytes 4194304 | tf_op jit(solution)/shard_map/pallas_call | solution.py:401
  60.0 0.0 collective-permute-done.5.refs_3_
  60.0 3.3 %shard_map.70.refs_2_ = f32[4,520,128]{2,1,0:T(8,128)S(1)} custom-call(s32[1]{0:T(128)} %bitcast.column_ref.refs_0_, f32[4,520,128]{2,1,0:T(8,128)S(1)} %maps.1.refs_1_, f32[4,520,128]{2,1,0:T(8,128)S(1)} %shard_map.69.refs_2_, bf16[4,528,128]{2,1,0:T(8,128)(2,1)S(1)} %collective-permute-done.5.refs_3_), custom_call_target="tpu_custom_call" | custom-call | flops 15974400 | bytes 4194304 | tf_op jit(solution)/shard_map/pallas_call | solution.py:401
  63.3 0.0 collective-permute-done.6.refs_3_
  63.3 4.1 %shard_map.71 = f32[64,16,128]{2,1,0:T(8,128)S(1)} custom-call(s32[1]{0:T(128)} %bitcast.column_ref.refs_0_, f32[4,520,128]{2,1,0:T(8,128)S(1)} %maps.1.refs_1_, f32[4,520,128]{2,1,0:T(8,128)S(1)} %shard_map.70.refs_2_, bf16[4,528,128]{2,1,0:T(8,128)(2,1)S(1)} %collective-permute-done.6.refs_3_), custom_call_target="tpu_custom_call" | custom-call | flops 15974400 | bytes 4194304 | tf_op jit(solution)/shard_map/pallas_call | solution.py:401
  67.4 37.4 %all_to_all.10 = f32[64,16,128]{2,1,0:T(8,128)S(1)} all-to-all(f32[64,16,128]{2,1,0:T(8,128)S(1)} %shard_map.71), channel_id=1, replica_groups=mesh['y'=8,'zl'=4,'c'=2,'zh'=2,'x'=4] {'y','zh','x'}, dimensions={0} | all-to-all | bytes 1048576 | tf_op jit(solution)/shard_map/all_to_all | solution.py:448
  104.8 0.1 reduce_sum.9
  104.9 0.6 slice_bitcast_fusion
  (1 shorter events, 0.0 us)
Async XLA Ops:
  6.7 9.0 %collective-permute-start.2 = (bf16[4,2,528,128]{3,2,1,0:T(8,128)(2,1)}, bf16[4,2,528,128]{3,2,1,0:T(8,128)(2,1)S(1)}, u32[]{:S(2)}, u32[]{:S(2)}) collective-permute-start(bf16[4,2,528,128]{3,2,1,0:T(8,128)(2,1)} %get-tuple-element.15), channel_id=1, source_target_pairs={{0,8},{8,0},{1,9},{9,1},{2,10},{10,2},{3,11},{11,3},{4,12},{12,4},... | collective-permute-start | bytes 3244040 | tf_op jit(solution)/shard_map/ppermute | solution.py:430
  8.6 26.2 %all-to-all-start = ((f32[8,136,128]{2,1,0:T(8,128)}), f32[8,136,128]{2,1,0:T(8,128)S(1)}, u32[]{:S(2)}, u32[]{:S(2)}) async-start(f32[8,136,128]{2,1,0:T(8,128)} %get-tuple-element.13), calls=%async_computation | async-start | bytes 1114112 | tf_op jit(solution)/shard_map/all_to_all | solution.py:437
  17.0 43.0 %collective-permute-start.5 = (bf16[4,528,128]{2,1,0:T(8,128)(2,1)}, bf16[4,528,128]{2,1,0:T(8,128)(2,1)S(1)}, u32[]{:S(2)}, u32[]{:S(2)}) collective-permute-start(bf16[4,528,128]{2,1,0:T(8,128)(2,1)} %get-tuple-element.22), channel_id=1, source_target_pairs={{0,16},{4,20},{8,24},{12,28},{16,32},{20,36},{24,40},{28,44},{32,4... | collective-permute-start | bytes 1622024 | tf_op jit(solution)/shard_map/ppermute | solution.py:30
  21.2 42.1 %collective-permute-start.6 = (bf16[4,528,128]{2,1,0:T(8,128)(2,1)}, bf16[4,528,128]{2,1,0:T(8,128)(2,1)S(1)}, u32[]{:S(2)}, u32[]{:S(2)}) collective-permute-start(bf16[4,528,128]{2,1,0:T(8,128)(2,1)} %get-tuple-element.23), channel_id=1, source_target_pairs={{0,52},{4,48},{8,60},{12,56},{16,0},{20,4},{24,8},{28,12},{32,16},... | collective-permute-start | bytes 1622024 | tf_op jit(solution)/shard_map/ppermute | solution.py:30
  23.2 33.5 %collective-permute-start.3 = (bf16[2,528,128]{2,1,0:T(8,128)(2,1)}, bf16[2,528,128]{2,1,0:T(8,128)(2,1)S(1)}, u32[]{:S(2)}, u32[]{:S(2)}) collective-permute-start(bf16[2,528,128]{2,1,0:T(8,128)(2,1)} %get-tuple-element.20), channel_id=1, source_target_pairs={{0,32},{4,36},{8,40},{12,44},{16,48},{20,52},{24,56},{28,60},{32,4... | collective-permute-start | bytes 811016 | tf_op jit(solution)/shard_map/ppermute | solution.py:30
  30.5 26.2 %collective-permute-start.4 = (bf16[2,528,128]{2,1,0:T(8,128)(2,1)}, bf16[2,528,128]{2,1,0:T(8,128)(2,1)S(1)}, u32[]{:S(2)}, u32[]{:S(2)}) collective-permute-start(bf16[2,528,128]{2,1,0:T(8,128)(2,1)} %get-tuple-element.21), channel_id=1, source_target_pairs={{0,36},{4,32},{8,44},{12,40},{16,52},{20,48},{24,60},{28,56},{32,0... | collective-permute-start | bytes 811016 | tf_op jit(solution)/shard_map/ppermute | solution.py:30
  35.4 9.6 %collective-permute-start.1 = (f32[3,8,128]{2,1,0:T(8,128)}, f32[3,8,128]{2,1,0:T(8,128)S(1)}, u32[]{:S(2)}, u32[]{:S(2)}) collective-permute-start(f32[3,8,128]{2,1,0:T(8,128)} %bitcast.16), channel_id=1, source_target_pairs={{8,0},{16,8},{24,16},{32,24},{40,32},{48,40},{56,48},{9,1},{17,9},... | collective-permute-start | bytes 36872 | tf_op jit(solution)/shard_map/ppermute | solution.py:36
  45.0 7.9 %collective-permute-start = (f32[3,8,128]{2,1,0:T(8,128)}, f32[3,8,128]{2,1,0:T(8,128)S(1)}, u32[]{:S(2)}, u32[]{:S(2)}) collective-permute-start(f32[3,8,128]{2,1,0:T(8,128)} %bitcast.16), channel_id=1, source_target_pairs={{0,8},{8,16},{16,24},{24,32},{32,40},{40,48},{48,56},{1,9},{9,17},... | collective-permute-start | bytes 36872 | tf_op jit(solution)/shard_map/ppermute | solution.py:36

commit v4 on v2

--- a/solution.py
+++ b/solution.py
@@ -24,7 +24,7 @@
     for low in range(CLASSES):
         for core in range(CORES):
             for high in range(HALVES):
-                z = (high * CLASSES + low + steps) % RING
+                z = (high * CLASSES + low + steps * (1 - 2 * core)) % RING
                 source = (low * CORES + core) * HALVES + high
                 pairs.append((source, ((z % CLASSES) * CORES + core) * HALVES + z // CLASSES))
     return lax.ppermute(value, ("zl", "c", "zh"), pairs)
@@ -56,8 +56,12 @@
     lax.fori_loop(0, dest_ref.shape[0], note, 0, unroll=4)
 
 
+def first_turn(core):
+    return 1 + core * (CLASSES - 2)
+
+
 def pack_kernel(
-    here_ref, dest_ref, params_ref, blocks_hbm, near_ref, right_ref, left_ref, right2_ref, left2_ref, other_ref,
+    here_ref, dest_ref, params_ref, blocks_hbm, near_ref, first_ref, second_ref, far_ref, other_ref,
     blocks_ref, sem, table, shifted, columns, rim, lines,
 ):
     number, tile_rows, tile_cols = blocks_ref.shape
@@ -69,6 +73,7 @@
     plain = turned(upright)[:number]
     for k in range(3):
         shifted[k] = plain if k == 0 else pltpu.roll(plain, k * PARAMS, 1)
+
     fetch.wait()
 
     lane8 = lax.broadcasted_iota(jnp.int32, (8, tile_cols), 1)
@@ -94,17 +99,18 @@
     count = CLASSES * CORES
     west_half = lax.broadcasted_iota(jnp.int32, (1, tile_cols), 1) < tile_rows
     pixels = ROWS * tile_rows
-    mine = {
-        0: (near_ref.at[0], near_ref.at[1]),
-        1: (right_ref.at[0], right_ref.at[1]),
-        2: (right2_ref.at[0], left2_ref.at[0]),
-        3: (left_ref.at[0], left_ref.at[1]),
-    }
+    turn = first_turn(core)
+    mine = [
+        (0, near_ref.at[0], near_ref.at[1]),
+        (turn, first_ref.at[0], first_ref.at[1]),
+        (CLASSES // 2, far_ref.at[core], far_ref.at[1 - core]),
+        (CLASSES - turn, second_ref.at[0], second_ref.at[1]),
+    ]
 
     for kind in range(CORES):
         for d in range(CLASSES):
-            column = ((low + d) % CLASSES) * CORES + (core + kind) % CORES
-            units = (other_ref.at[d, 0], other_ref.at[d, 1]) if kind else mine[d]
+            step, *units = (d, other_ref.at[d, 0], other_ref.at[d, 1]) if kind else mine[d]
+            column = ((low + step) % CLASSES) * CORES + (core + kind) % CORES
 
             def place(step, carry):
                 found = []
@@ -142,9 +148,9 @@
     unit = (ROWS * tile_rows + 2 * ROWS, tile_cols)
     return pl.pallas_call(
         pack_kernel,
-        out_shape=[pltpu.VMEM(lead + unit, jnp.bfloat16) for lead in ((2,), (2,), (2,), (1,), (1,), (CLASSES, 2))],
+        out_shape=[pltpu.VMEM(lead + unit, jnp.bfloat16) for lead in ((2,), (2,), (2,), (2,), (CLASSES, 2))],
         in_specs=[SMEM, SMEM, VMEM, pl.BlockSpec(memory_space=pltpu.HBM)],
-        out_specs=[VMEM] * 6,
+        out_specs=[VMEM] * 5,
         scratch_shapes=[
             pltpu.VMEM(blocks.shape, jnp.bfloat16),
             pltpu.SemaphoreType.DMA,
@@ -160,26 +166,50 @@
     )(here, *[pltpu.with_memory_space_constraint(a, pltpu.HBM) for a in (dest, params, blocks)])
 
 
-def join_kernel(swapped_ref, *refs):
-    own, (right_ref, left_ref, right2_ref, left2_ref) = refs[:4], refs[4:]
-    for half, some in zip((right_ref, left_ref, right2_ref, left2_ref), own):
-        half[: some.shape[0]] = some[...]
-    right_ref[2:4] = swapped_ref[1]
-    left_ref[2:4] = swapped_ref[3]
-    right2_ref[1] = swapped_ref[2, 0]
-    left2_ref[1] = swapped_ref[2, 1]
-
-
-def join(swapped, *own):
+def join_kernel(here_ref, swapped_ref, first_own, second_own, far_own, first_ref, second_ref, far0_ref, far1_ref):
+    core = here_ref[1]
+    turn = first_turn(core)
+    first_ref[0:2] = first_own[...]
+    first_ref[2:4] = swapped_ref[turn]
+    second_ref[0:2] = second_own[...]
+    second_ref[2:4] = swapped_ref[CLASSES - turn]
+    far0_ref[0] = far_own[0]
+    far0_ref[1] = swapped_ref[CLASSES // 2, core]
+    far1_ref[0] = far_own[1]
+    far1_ref[1] = swapped_ref[CLASSES // 2, 1 - core]
+
+
+def join(here, swapped, *own):
+    unit = swapped.shape[2:]
     return pl.pallas_call(
         join_kernel,
-        out_shape=[pltpu.VMEM((2 * a.shape[0],) + a.shape[1:], a.dtype) for a in own],
-        in_specs=[VMEM] * 5,
+        out_shape=[pltpu.VMEM((n,) + unit, swapped.dtype) for n in (4, 4, 2, 2)],
+        in_specs=[SMEM] + [VMEM] * 4,
         out_specs=[VMEM] * 4,
         cost_estimate=pl.CostEstimate(flops=0, bytes_accessed=2 << 20, transcendentals=0),
         compiler_params=pltpu.CompilerParams(vmem_limit_bytes=4 << 20),
         name="join",
-    )(*in_vmem(swapped, *own))
+    )(here, *in_vmem(swapped, *own))
+
+
+def copies_kernel(height_ref, albedo_ref, rows_ref, out_ref):
+    tile_rows = height_ref.shape[0]
+    for row in range(ROWS):
+        out_ref[row, :tile_rows, :] = height_ref[...]
+        out_ref[row, tile_rows : 2 * tile_rows, :] = albedo_ref[...]
+        out_ref[row, 2 * tile_rows :, :] = rows_ref[...]
+
+
+def make_copies(height, albedo, rows):
+    return pl.pallas_call(
+        copies_kernel,
+        out_shape=pltpu.VMEM((ROWS, 2 * height.shape[0] + ROWS, height.shape[1]), jnp.float32),
+        in_specs=[VMEM] * 3,
+        out_specs=VMEM,
+        cost_estimate=pl.CostEstimate(flops=0, bytes_accessed=1 << 20, transcendentals=0),
+        compiler_params=pltpu.CompilerParams(vmem_limit_bytes=4 << 20),
+        name="copies",
+    )(*in_vmem(height, albedo, rows))
 
 
 def turned(rows):
@@ -402,6 +432,11 @@
     tile_rows, tile_cols = heights.shape[1:]
     block_count = block_dest.shape[2]
 
+    height, shade = heights[0], albedo[0]
+    first, last = jnp.stack([height[:, 0], height[:, 1], shade[:, 0]]), jnp.stack([height[:, -1], height[:, -2], shade[:, -1]])
+    from_west = column_shift(last, 1)
+    from_east = column_shift(first, -1)
+
     here = jnp.stack([lax.axis_index("zl"), lax.axis_index("c")]).astype(jnp.int32)
     near, *own, other = pack(
         here,
@@ -410,27 +445,24 @@
         blocks.reshape(block_count, tile_rows, tile_cols),
     )
     swapped = lax.ppermute(other, "c", [(0, 1), (1, 0)])
-    to_right, to_left, to_right2, to_left2 = join(swapped, *own)
-    right2 = ring_shift(to_right2, 2)
-    left2 = ring_shift(to_left2, -2)
-    right = ring_shift(to_right, 1)
-    left = ring_shift(to_left, -1)
-
-    height, shade = heights[0], albedo[0]
-    first, last = jnp.stack([height[:, 0], height[:, 1], shade[:, 0]]), jnp.stack([height[:, -1], height[:, -2], shade[:, -1]])
-    from_west = column_shift(last, 1)
-    from_east = column_shift(first, -1)
+    to_first, to_second, to_far0, to_far1 = join(here, swapped, *own)
+    far0 = ring_shift(to_far0, 2)
+    far1 = ring_shift(to_far1, -2)
+    next0 = ring_shift(to_first, 1)
+    next1 = ring_shift(to_second, -1)
+
     beside = jnp.concatenate([from_west, from_east], axis=1)
     mine = jnp.concatenate([first[:1], last[:1]], axis=1)
     rows = jnp.concatenate([beside, mine, jnp.zeros((ROWS - 4, tile_cols), jnp.float32)])
-    copies = jnp.broadcast_to(jnp.concatenate([height, shade, rows])[None], (ROWS, 2 * tile_rows + ROWS, tile_cols))
+    copies = make_copies(height, shade, rows)
     gathered = lax.all_to_all(copies, "y", split_axis=0, concat_axis=0, tiled=True)
     column = column_here.reshape(1).astype(jnp.int32)
     maps = make_maps(column, gathered)
 
     sums = terms(column, maps, None, [(near, [(0,), (1,)]), (swapped, [(0, 0), (0, 1)])], None)
-    sums = terms(column, maps, sums, [(right2, EACH2), (left2, EACH2)], None)
-    parts = terms(column, maps, sums, [(right, EACH4), (left, EACH4)], 1.0 / block_count)
+    sums = terms(column, maps, sums, [(far0, EACH2), (far1, EACH2)], None)
+    sums = terms(column, maps, sums, [(next0, EACH4)], None)
+    parts = terms(column, maps, sums, [(next1, EACH4)], 1.0 / block_count)
     summed = jnp.sum(lax.all_to_all(parts, ("y",) + IMG, split_axis=0, concat_axis=0, tiled=True), axis=0)
     half = tile_rows // (HALVES * DEPTH)
     return (summed[None, :half], summed[None, half:])

time: 108 us -> 106 us (0.981)
  Pallas kernels: 20.4 us -> 22.7 us
  waiting for transfers between devices: 13.6 us -> 11.7 us
  blocking collectives: 37.3 us -> 35.8 us
    ppermute x4, waiting for transfers between devices: 10.4 us -> 8.5 us  [ring_shift(): return lax.ppermute(value, ('zl', 'c', 'zh'), pairs)]
    all_to_all x1, blocking collectives: 37.3 us -> 35.8 us  [body(): lax.all_to_all(parts, ('y',) + IMG, split_axis=0, concat_axis=0, tiled=True)]
    pallas_call x1 -> x2, Pallas kernels: 1.3 us -> 2.7 us  [the longest x1 1.84 us: join(): pl.pallas_call(join_kernel, out_shape=[pltpu.VMEM((n,) + unit, swapped.dt...]
    pallas_call x3 -> x4, Pallas kernels: 13 us -> 14 us  [terms(): pl.pallas_call(lambda *refs: terms_kernel(scale, sums is not None, picks,...]
  transfers between devices with their start and end apart: 8 -> 8, of which waited for: 3 -> 3; matrix products, arithmetic and copies ran while one was open for 1% -> 1% of each run, Pallas kernels for 8% -> 12%
where the time goes in v4:
time: 106 us
  blocking collectives  35.8 us (34%)
  starting transfers between devices  33.4 us (32%)
  Pallas kernels  22.7 us (21%)
  waiting for transfers between devices  11.7 us (11%)
  local copies, waits for them, and re-layouts  1.08 us (1%)
    all_to_all x1, blocking collectives, body(): lax.all_to_all(parts, ('y',) + IMG, split_axis=0, concat_axis=0, tiled=True)  35.8 us
    ppermute x4, starting transfers between devices, ring_shift(): return lax.ppermute(value, ('zl', 'c', 'zh'), pairs)  20.7 us
    pallas_call x4, Pallas kernels, terms(): pl.pallas_call(lambda *refs: terms_kernel(scale, sums is not None, picks,...  14 us
    ppermute x4, waiting for transfers between devices, ring_shift(): return lax.ppermute(value, ('zl', 'c', 'zh'), pairs)  8.5 us
    all_to_all x1, starting transfers between devices, body(): lax.all_to_all(copies, 'y', split_axis=0, concat_axis=0, tiled=True)  7.1 us
    pallas_call x1, Pallas kernels, pack(): pl.pallas_call(pack_kernel, out_shape=[pltpu.VMEM(lead + unit, jnp.bfloat...  5.65 us
    ppermute x2, starting transfers between devices, column_shift(): return lax.ppermute(value, ('zl', 'c'), pairs)  3.69 us
    ppermute x2, waiting for transfers between devices, column_shift(): return lax.ppermute(value, ('zl', 'c'), pairs)  3.17 us
  transfers between devices with their start and end apart: 8, of which 3 were waited for; matrix products, arithmetic and copies ran while one was open for 1% of the time, Pallas kernels for 12%

profile of v4, /device:TPU:6, one launch (start us, length us, event | category | flops | bytes accessed | tf_op | source)
XLA Modules:
  0.0 105.8 jit_solution(4046641934879648846)
XLA Ops:
  0.7 0.1 pad_add_fusion.here_ref
  0.7 5.6 %pack.1 = (bf16[2,528,128]{2,1,0:T(8,128)(2,1)S(1)}, bf16[2,528,128]{2,1,0:T(8,128)(2,1)S(1)}, bf16[2,528,128]{2,1,0:T(8,128)(2,1)S(1)}, bf16[2,528,128]{2,1,0:T(8,128)(2,1)S(1)}, bf16[4,2,528,128]{3,2,1,0:T(8,128)(2,1)}) custom-call(s32[2]{0:T(128)S(1)} %pad_add_fusion.here_ref, s32[64]{0:T(128)} %bitcast.34, bf16[8,64]{1,0:T(8,128)(2,1)} %bitcast.29, ...), custom_call_target="tpu_custom_call" | custom-call | bytes 6291456 | tf_op jit(solution)/shard_map/pack/pallas_call | solution.py:149
  6.4 1.9 %collective-permute-start.2 = (bf16[4,2,528,128]{3,2,1,0:T(8,128)(2,1)}, bf16[4,2,528,128]{3,2,1,0:T(8,128)(2,1)S(1)}, u32[]{:S(2)}, u32[]{:S(2)}) collective-permute-start(bf16[4,2,528,128]{3,2,1,0:T(8,128)(2,1)} %get-tuple-element.12), channel_id=1, source_target_pairs={{0,8},{8,0},{1,9},{9,1},{2,10},{10,2},{3,11},{11,3},{4,12},{12,4},... | collective-permute-start | bytes 3244040 | tf_op jit(solution)/shard_map/ppermute | solution.py:447
  8.3 0.2 slice_reduce_fusion.3
  8.5 0.2 slice_reduce_fusion.4
  8.8 2.4 %collective-permute-start = (f32[3,64]{1,0:T(4,128)S(1)}, f32[3,64]{1,0:T(4,128)S(1)}, u32[]{:S(2)}, u32[]{:S(2)}) collective-permute-start(f32[3,64]{1,0:T(4,128)S(1)} %pad_maximum_fusion), channel_id=1, source_target_pairs={{0,8},{8,16},{16,24},{24,32},{32,40},{40,48},{48,56},{1,9},{9,17},... | collective-permute-start | bytes 2312 | tf_op jit(solution)/shard_map/ppermute | solution.py:36
  11.2 1.3 %collective-permute-start.1 = (f32[3,64]{1,0:T(4,128)S(1)}, f32[3,64]{1,0:T(4,128)S(1)}, u32[]{:S(2)}, u32[]{:S(2)}) collective-permute-start(f32[3,64]{1,0:T(4,128)S(1)} %pad_maximum_fusion.1), channel_id=1, source_target_pairs={{8,0},{16,8},{24,16},{32,24},{40,32},{48,40},{56,48},{9,1},{17,9},... | collective-permute-start | bytes 2312 | tf_op jit(solution)/shard_map/ppermute | solution.py:36
  12.5 0.1 pad.6.clone
  12.6 0.0 collective-permute-done
  12.6 3.2 %collective-permute-done.1 = f32[3,64]{1,0:T(4,128)S(1)} collective-permute-done((f32[3,64]{1,0:T(4,128)S(1)}, f32[3,64]{1,0:T(4,128)S(1)}, u32[]{:S(2)}, u32[]{:S(2)}) %collective-permute-start.1) | collective-permute-done | bytes 800 | tf_op jit(solution)/shard_map/ppermute | solution.py:36
  15.7 0.1 maximum_maximum_fusion.rows_ref
  15.8 0.9 copies.1
  16.7 7.1 %all-to-all-start = ((f32[8,136,128]{2,1,0:T(8,128)}), f32[8,136,128]{2,1,0:T(8,128)S(1)}, u32[]{:S(2)}, u32[]{:S(2)}) async-start(f32[8,136,128]{2,1,0:T(8,128)} %copies.1), calls=%async_computation | async-start | bytes 1114112 | tf_op jit(solution)/shard_map/all_to_all | solution.py:458
  23.8 0.0 collective-permute-done.2.refs_3_.swapped_ref
  23.8 1.8 %join.1 = (bf16[4,528,128]{2,1,0:T(8,128)(2,1)}, bf16[4,528,128]{2,1,0:T(8,128)(2,1)}, bf16[2,528,128]{2,1,0:T(8,128)(2,1)}, bf16[2,528,128]{2,1,0:T(8,128)(2,1)}) custom-call(s32[2]{0:T(128)S(1)} %pad_add_fusion.here_ref, bf16[4,2,528,128]{3,2,1,0:T(8,128)(2,1)S(1)} %collective-permute-done.2.refs_3_.swapped_ref, ...), custom_call_target="tpu_custom_call" | custom-call | bytes 2097152 | tf_op jit(solution)/shard_map/join/pallas_call | solution.py:184
  25.6 4.3 %collective-permute-start.5 = (bf16[4,528,128]{2,1,0:T(8,128)(2,1)}, bf16[4,528,128]{2,1,0:T(8,128)(2,1)S(1)}, u32[]{:S(2)}, u32[]{:S(2)}) collective-permute-start(bf16[4,528,128]{2,1,0:T(8,128)(2,1)} %get-tuple-element.18), channel_id=1, source_target_pairs={{0,16},{4,20},{8,60},{12,56},{16,32},{20,36},{24,8},{28,12},{32,48... | collective-permute-start | bytes 1622024 | tf_op jit(solution)/shard_map/ppermute | solution.py:30
  29.9 8.5 %collective-permute-start.6 = (bf16[4,528,128]{2,1,0:T(8,128)(2,1)}, bf16[4,528,128]{2,1,0:T(8,128)(2,1)S(1)}, u32[]{:S(2)}, u32[]{:S(2)}) collective-permute-start(bf16[4,528,128]{2,1,0:T(8,128)(2,1)} %get-tuple-element.19), channel_id=1, source_target_pairs={{0,52},{4,48},{8,24},{12,28},{16,0},{20,4},{24,40},{28,44},{32,16}... | collective-permute-start | bytes 1622024 | tf_op jit(solution)/shard_map/ppermute | solution.py:30
  38.4 1.9 %collective-permute-start.3 = (bf16[2,528,128]{2,1,0:T(8,128)(2,1)}, bf16[2,528,128]{2,1,0:T(8,128)(2,1)S(1)}, u32[]{:S(2)}, u32[]{:S(2)}) collective-permute-start(bf16[2,528,128]{2,1,0:T(8,128)(2,1)} %get-tuple-element.16), channel_id=1, source_target_pairs={{0,32},{4,36},{8,44},{12,40},{16,48},{20,52},{24,60},{28,56},{32,4... | collective-permute-start | bytes 811016 | tf_op jit(solution)/shard_map/ppermute | solution.py:30
  40.3 6.0 %collective-permute-start.4 = (bf16[2,528,128]{2,1,0:T(8,128)(2,1)}, bf16[2,528,128]{2,1,0:T(8,128)(2,1)S(1)}, u32[]{:S(2)}, u32[]{:S(2)}) collective-permute-start(bf16[2,528,128]{2,1,0:T(8,128)(2,1)} %get-tuple-element.17), channel_id=1, source_target_pairs={{0,36},{4,32},{8,40},{12,44},{16,52},{20,48},{24,56},{28,60},{32,0... | collective-permute-start | bytes 811016 | tf_op jit(solution)/shard_map/ppermute | solution.py:30
  46.4 0.0 all-to-all-done.got_ref
  46.4 0.4 maps.1.refs_1_
  46.8 3.3 %shard_map.68.refs_2_ = f32[4,520,128]{2,1,0:T(8,128)S(1)} custom-call(s32[1]{0:T(128)} %bitcast.column_ref.refs_0_, f32[4,520,128]{2,1,0:T(8,128)S(1)} %maps.1.refs_1_, bf16[2,528,128]{2,1,0:T(8,128)(2,1)S(1)} %get-tuple-element.11.refs_2_, bf16[4,2,528,128]{3,2,1,0:T(8,128)(2,1)S(1)} %collective-permute-done.2.refs_3_.swapped_ref), custom_call_target="tpu_custom_call" | custom-call | flops 15974400 | bytes 4194304 | tf_op jit(solution)/shard_map/pallas_call | solution.py:415
  50.1 6.8 %collective-permute-done.3.refs_3_ = bf16[2,528,128]{2,1,0:T(8,128)(2,1)S(1)} collective-permute-done((bf16[2,528,128]{2,1,0:T(8,128)(2,1)}, bf16[2,528,128]{2,1,0:T(8,128)(2,1)S(1)}, u32[]{:S(2)}, u32[]{:S(2)}) %collective-permute-start.3) | collective-permute-done | bytes 270368 | tf_op jit(solution)/shard_map/ppermute | solution.py:30
  56.9 1.7 %collective-permute-done.4.refs_4_ = bf16[2,528,128]{2,1,0:T(8,128)(2,1)S(1)} collective-permute-done((bf16[2,528,128]{2,1,0:T(8,128)(2,1)}, bf16[2,528,128]{2,1,0:T(8,128)(2,1)S(1)}, u32[]{:S(2)}, u32[]{:S(2)}) %collective-permute-start.4) | collective-permute-done | bytes 270368 | tf_op jit(solution)/shard_map/ppermute | solution.py:30
  58.6 3.3 %shard_map.69.refs_2_ = f32[4,520,128]{2,1,0:T(8,128)S(1)} custom-call(s32[1]{0:T(128)} %bitcast.column_ref.refs_0_, f32[4,520,128]{2,1,0:T(8,128)S(1)} %maps.1.refs_1_, f32[4,520,128]{2,1,0:T(8,128)S(1)} %shard_map.68.refs_2_, bf16[2,528,128]{2,1,0:T(8,128)(2,1)S(1)} %collective-permute-done.3.refs_3_, bf16[2,528,128]{2,1,0:T(8,128)(2,1)S(1)} %collective-permute-done.4.refs_4_), custom_call_target="tpu_custom_call" | custom-call | flops 15974400 | bytes 4194304 | tf_op jit(solution)/shard_map/pallas_call | solution.py:415
  61.9 0.0 collective-permute-done.5.refs_3_
  61.9 3.3 %shard_map.70.refs_2_ = f32[4,520,128]{2,1,0:T(8,128)S(1)} custom-call(s32[1]{0:T(128)} %bitcast.column_ref.refs_0_, f32[4,520,128]{2,1,0:T(8,128)S(1)} %maps.1.refs_1_, f32[4,520,128]{2,1,0:T(8,128)S(1)} %shard_map.69.refs_2_, bf16[4,528,128]{2,1,0:T(8,128)(2,1)S(1)} %collective-permute-done.5.refs_3_), custom_call_target="tpu_custom_call" | custom-call | flops 15974400 | bytes 4194304 | tf_op jit(solution)/shard_map/pallas_call | solution.py:415
  65.2 0.0 collective-permute-done.6.refs_3_
  65.2 4.1 %shard_map.71 = f32[64,16,128]{2,1,0:T(8,128)S(1)} custom-call(s32[1]{0:T(128)} %bitcast.column_ref.refs_0_, f32[4,520,128]{2,1,0:T(8,128)S(1)} %maps.1.refs_1_, f32[4,520,128]{2,1,0:T(8,128)S(1)} %shard_map.70.refs_2_, bf16[4,528,128]{2,1,0:T(8,128)(2,1)S(1)} %collective-permute-done.6.refs_3_), custom_call_target="tpu_custom_call" | custom-call | flops 15974400 | bytes 4194304 | tf_op jit(solution)/shard_map/pallas_call | solution.py:415
  69.3 35.8 %all_to_all.10 = f32[64,16,128]{2,1,0:T(8,128)S(1)} all-to-all(f32[64,16,128]{2,1,0:T(8,128)S(1)} %shard_map.71), channel_id=1, replica_groups=mesh['y'=8,'zl'=4,'c'=2,'zh'=2,'x'=4] {'y','zh','x'}, dimensions={0} | all-to-all | bytes 1048576 | tf_op jit(solution)/shard_map/all_to_all | solution.py:466
  105.1 0.1 reduce_sum.9
  105.2 0.6 slice_bitcast_fusion
  (7 shorter events, 0.0 us)
Async XLA Ops:
  0.6 7.7 %copy-start.1 = (f32[1,64,128]{2,1,0:T(8,128)S(1)}, f32[1,64,128]{2,1,0:T(8,128)}, u32[]{:S(2)}) copy-start(f32[1,64,128]{2,1,0:T(8,128)} %param.6) | copy-start | bytes 98308
  0.6 7.9 %copy-start = (f32[1,64,128]{2,1,0:T(8,128)S(1)}, f32[1,64,128]{2,1,0:T(8,128)}, u32[]{:S(2)}) copy-start(f32[1,64,128]{2,1,0:T(8,128)} %param.5) | copy-start | bytes 98308
  6.4 17.4 %collective-permute-start.2 = (bf16[4,2,528,128]{3,2,1,0:T(8,128)(2,1)}, bf16[4,2,528,128]{3,2,1,0:T(8,128)(2,1)S(1)}, u32[]{:S(2)}, u32[]{:S(2)}) collective-permute-start(bf16[4,2,528,128]{3,2,1,0:T(8,128)(2,1)} %get-tuple-element.12), channel_id=1, source_target_pairs={{0,8},{8,0},{1,9},{9,1},{2,10},{10,2},{3,11},{11,3},{4,12},{12,4},... | collective-permute-start | bytes 3244040 | tf_op jit(solution)/shard_map/ppermute | solution.py:447
  8.8 3.8 %collective-permute-start = (f32[3,64]{1,0:T(4,128)S(1)}, f32[3,64]{1,0:T(4,128)S(1)}, u32[]{:S(2)}, u32[]{:S(2)}) collective-permute-start(f32[3,64]{1,0:T(4,128)S(1)} %pad_maximum_fusion), channel_id=1, source_target_pairs={{0,8},{8,16},{16,24},{24,32},{32,40},{40,48},{48,56},{1,9},{9,17},... | collective-permute-start | bytes 2312 | tf_op jit(solution)/shard_map/ppermute | solution.py:36
  11.2 4.6 %collective-permute-start.1 = (f32[3,64]{1,0:T(4,128)S(1)}, f32[3,64]{1,0:T(4,128)S(1)}, u32[]{:S(2)}, u32[]{:S(2)}) collective-permute-start(f32[3,64]{1,0:T(4,128)S(1)} %pad_maximum_fusion.1), channel_id=1, source_target_pairs={{8,0},{16,8},{24,16},{32,24},{40,32},{48,40},{56,48},{9,1},{17,9},... | collective-permute-start | bytes 2312 | tf_op jit(solution)/shard_map/ppermute | solution.py:36
  16.7 29.7 %all-to-all-start = ((f32[8,136,128]{2,1,0:T(8,128)}), f32[8,136,128]{2,1,0:T(8,128)S(1)}, u32[]{:S(2)}, u32[]{:S(2)}) async-start(f32[8,136,128]{2,1,0:T(8,128)} %copies.1), calls=%async_computation | async-start | bytes 1114112 | tf_op jit(solution)/shard_map/all_to_all | solution.py:458
  25.6 36.3 %collective-permute-start.5 = (bf16[4,528,128]{2,1,0:T(8,128)(2,1)}, bf16[4,528,128]{2,1,0:T(8,128)(2,1)S(1)}, u32[]{:S(2)}, u32[]{:S(2)}) collective-permute-start(bf16[4,528,128]{2,1,0:T(8,128)(2,1)} %get-tuple-element.18), channel_id=1, source_target_pairs={{0,16},{4,20},{8,60},{12,56},{16,32},{20,36},{24,8},{28,12},{32,48... | collective-permute-start | bytes 1622024 | tf_op jit(solution)/shard_map/ppermute | solution.py:30
  29.9 35.3 %collective-permute-start.6 = (bf16[4,528,128]{2,1,0:T(8,128)(2,1)}, bf16[4,528,128]{2,1,0:T(8,128)(2,1)S(1)}, u32[]{:S(2)}, u32[]{:S(2)}) collective-permute-start(bf16[4,528,128]{2,1,0:T(8,128)(2,1)} %get-tuple-element.19), channel_id=1, source_target_pairs={{0,52},{4,48},{8,24},{12,28},{16,0},{20,4},{24,40},{28,44},{32,16}... | collective-permute-start | bytes 1622024 | tf_op jit(solution)/shard_map/ppermute | solution.py:30
  38.4 18.5 %collective-permute-start.3 = (bf16[2,528,128]{2,1,0:T(8,128)(2,1)}, bf16[2,528,128]{2,1,0:T(8,128)(2,1)S(1)}, u32[]{:S(2)}, u32[]{:S(2)}) collective-permute-start(bf16[2,528,128]{2,1,0:T(8,128)(2,1)} %get-tuple-element.16), channel_id=1, source_target_pairs={{0,32},{4,36},{8,44},{12,40},{16,48},{20,52},{24,60},{28,56},{32,4... | collective-permute-start | bytes 811016 | tf_op jit(solution)/shard_map/ppermute | solution.py:30
  40.3 18.3 %collective-permute-start.4 = (bf16[2,528,128]{2,1,0:T(8,128)(2,1)}, bf16[2,528,128]{2,1,0:T(8,128)(2,1)S(1)}, u32[]{:S(2)}, u32[]{:S(2)}) collective-permute-start(bf16[2,528,128]{2,1,0:T(8,128)(2,1)} %get-tuple-element.17), channel_id=1, source_target_pairs={{0,36},{4,32},{8,40},{12,44},{16,52},{20,48},{24,56},{28,60},{32,0... | collective-permute-start | bytes 811016 | tf_op jit(solution)/shard_map/ppermute | solution.py:30
